TPU v7x, 128 devices: a whole 4x4x4 slice. The times are simulated.
128 devices in a mesh: rep: 16 (over z_hi, x, core), sp: 8 (over z_lo, y).
Axes of the slice: x: 4, y: 4, z: 4 (z_hi: 2, z_lo: 2; z = z_hi * 2 + z_lo), core: 2. Of those that a mesh axis runs over, the one named last changes fastest.
Arguments:
- positions: float32 [16, 3, 65536], P('rep', None, 'sp'), may hold values from -18 to 18
- velocities: float32 [16, 3, 65536], P('rep', None, 'sp'), may hold values from -6 to 6
- strength: float32 [16, 65536], P('rep', 'sp'), may hold values from 0.5 to 2
- inv_mass: float32 [16, 65536], P('rep', 'sp'), may hold values from 0.1 to 1
- tile_lists: int32 [16, 4, 512, 4], P('rep', None, 'sp'), may hold values from 0 to 127, as said below
- solute_index: int32 [16, 2048], P('rep', 'sp'), may hold values from 0 to 8191, as said below
- scatter_weight: float32 [16, 2048], P('rep', 'sp'), may hold values from 0.3 to 3
- intensity_exp: float32 [48], replicated, may hold values from 0.5 to 3
- precision: float32 [48], replicated, may hold values from 1 to 4
Outputs:
- positions_out: float32 [16, 3, 65536], P('rep', None, 'sp')
- velocities_out: float32 [16, 3, 65536], P('rep', None, 'sp')
Inputs may be any that keep to these rules, and one draw needn't show every extreme that they name: `tile_lists`: for each replica, step and local block b of a domain (numbered 0 to 63), the 4 entries are distinct extended block numbers from b to b + 64, among them b, b + 32 and b + 64. `solute_index`: within each replica and domain the 256 entries are distinct local atom numbers.
All inputs are finite; a program needn't handle non-finite values.
Results may differ from a plain program's by a relative error of at most 0.0001.
Values sent between devices are 32-bit elements; how exact they have to be, the bound alone decides.
No kernel may reach another device: no remote copies, remote signals or barrier semaphores. Data moves between devices by JAX's collectives and lax.ppermute only.
A program may use at most 128 MiB of HBM per device.

v0:
```python
import math

import jax
import jax.numpy as jnp
from jax import lax
from jax.sharding import PartitionSpec as P

M = 784
OUTER = 2
INNER = 2


TIME_STEP = 0.05
PAIR_STRENGTH = 0.2
HALF_INVERSE = 0.03125
shell_batch = 8
group_limit = 8


def extended_2(cells, sides, width):
    for axis, dim in sides:
        count = lax.axis_size(axis)
        ends = count - 1
        head = lax.slice_in_dim(cells, 0, width, axis=dim)
        tail = lax.slice_in_dim(cells, cells.shape[dim] - width, cells.shape[dim], axis=dim)
        cells = jnp.concatenate(
            [
                lax.ppermute(tail, axis, [(i, (i + 1) % count) for i in range(ends)]),
                cells,
                lax.ppermute(head, axis, [((i + 1) % count, i) for i in range(ends)]),
            ],
            axis=dim,
        )
    return cells


def directions(total_terms):
    order_index = jnp.arange(total_terms, dtype=jnp.int32)
    height = 1.0 - (2.0 * order_index.astype(jnp.float32) + 1.0) / total_terms
    radius = jnp.sqrt(1.0 - height * height)
    azimuth = (order_index * 610 % 987).astype(jnp.float32) * (2.0 * math.pi / 987.0)
    return (radius * jnp.cos(azimuth), radius * jnp.sin(azimuth), height)


def shell_values(total_shells):
    return 1.0 + 3.0 * jnp.arange(total_shells, dtype=jnp.int32).astype(jnp.float32) / total_shells


def projection(points, dir_x, dir_y, dir_z):
    return (
        dir_x[:, None] * points[0][None, :]
        + dir_y[:, None] * points[1][None, :]
        + dir_z[:, None] * points[2][None, :]
    )


def amplitude_terms(project, weights, shell_q):
    shell_blocks = shell_q.reshape(-1, shell_batch)

    def one_block(shell_block):
        phases = shell_block[:, None, None] * project[None]
        return jnp.stack(
            [
                jnp.sum(weights * jnp.cos(phases), axis=-1),
                jnp.sum(weights * jnp.sin(phases), axis=-1),
            ]
        )

    result = lax.map(one_block, shell_blocks)
    return jnp.transpose(result, (1, 0, 2, 3)).reshape(2, -1, project.shape[0])


def shell_intensity(amplitude):
    return jnp.mean(amplitude[0] * amplitude[0] + amplitude[1] * amplitude[1], axis=-1)


def scale_grad(amplitude, intensity, precision, intensity_exp, total_terms):
    coef_shell = 2.0 * precision * (intensity - intensity_exp) / total_terms
    return coef_shell[None, :, None] * amplitude


def restraint_forces(project, weights, shell_q, weight_grad, dir_x, dir_y, dir_z):
    shell_blocks = shell_q.reshape(-1, shell_batch)
    grad_real = weight_grad[0].reshape(-1, shell_batch, project.shape[0])
    grad_imag = weight_grad[1].reshape(-1, shell_batch, project.shape[0])

    def add_block(running, pieces):
        shell_block, block_real, block_imag = pieces
        phases = shell_block[:, None, None] * project[None]
        block_term = jnp.sum(
            shell_block[:, None, None]
            * (block_imag[:, :, None] * jnp.cos(phases) - block_real[:, :, None] * jnp.sin(phases)),
            axis=0,
        )
        return (running + block_term, None)

    running, unused = lax.scan(
        add_block, jnp.zeros(project.shape, jnp.float32), (shell_blocks, grad_real, grad_imag)
    )
    return jnp.stack(
        [
            -weights * jnp.sum(dir_x[:, None] * running, axis=0),
            -weights * jnp.sum(dir_y[:, None] * running, axis=0),
            -weights * jnp.sum(dir_z[:, None] * running, axis=0),
        ]
    )


def pair_group(own_rows, near_rows, coupling):
    delta_list = [
        own_rows[component][:, :, None] - near_rows[component][:, None, :] for component in range(3)
    ]
    distance = (
        delta_list[0] * delta_list[0]
        + delta_list[1] * delta_list[1]
        + delta_list[2] * delta_list[2]
    )
    pair_weight = (
        coupling
        * own_rows[3][:, :, None]
        * near_rows[3][:, None, :]
        * jnp.exp(-HALF_INVERSE * distance)
    )
    return jnp.stack([jnp.sum(pair_weight * delta, axis=-1) for delta in delta_list])


def pair_forces(own_blocks, ext_blocks, tile_list):
    block_count, neighbours = tile_list.shape
    block_width = own_blocks.shape[2]
    group_size = min(group_limit, block_count)
    coupling = PAIR_STRENGTH / math.sqrt(neighbours * block_width)
    nearby = jnp.take(ext_blocks, tile_list.reshape(-1), axis=1).reshape(
        4, block_count // group_size, group_size, neighbours * block_width
    )
    grouped = own_blocks.reshape(4, block_count // group_size, group_size, block_width)

    def one_group(pieces):
        return pair_group(pieces[0], pieces[1], coupling)

    result = lax.map(one_group, (jnp.moveaxis(grouped, 1, 0), jnp.moveaxis(nearby, 1, 0)))
    return jnp.moveaxis(result, 0, 1).reshape(3, -1)


def shards(
    positions,
    velocities,
    strength,
    inv_mass,
    tile_lists,
    solute_index,
    scatter_weight,
    intensity_exp,
    precision,
):
    coords_now = positions[0]
    speed_now = velocities[0]
    charge = strength[0]
    inverse = inv_mass[0]
    solute_slots = solute_index[0]
    weights = scatter_weight[0]
    atom_dev = coords_now.shape[1]
    rim_width = atom_dev // 2
    block_width = 128
    replica_count = lax.axis_size("rep")
    scale_norm = 1.0 / math.sqrt(lax.axis_size("sp") * solute_slots.shape[0])
    dir_x, dir_y, dir_z = directions(M)
    shell_q = shell_values(intensity_exp.shape[0])
    mass_here = inverse[solute_slots]
    for outer_step in range(OUTER):
        points = jnp.take(coords_now, solute_slots, axis=1)
        project = projection(points, dir_x, dir_y, dir_z)
        partial_value = amplitude_terms(project, weights, shell_q) * scale_norm
        amplitude = lax.psum(partial_value, "sp")
        intensity = lax.psum(shell_intensity(amplitude), "rep") / replica_count
        weight_grad = scale_grad(amplitude, intensity, precision, intensity_exp, M)
        saxs_kick = restraint_forces(project, weights, shell_q, weight_grad, dir_x, dir_y, dir_z)
        for inner_step in range(INNER):
            tile_list = tile_lists[0, outer_step * INNER + inner_step]
            rows_all = jnp.concatenate([coords_now, charge[None, :]], axis=0)
            extended = extended_2(rows_all, (("sp", 1),), rim_width)
            own_blocks = rows_all.reshape(4, atom_dev // block_width, block_width)
            ext_blocks = extended.reshape(4, extended.shape[1] // block_width, block_width)
            pair_push = pair_forces(own_blocks, ext_blocks, tile_list)
            speed_now = speed_now + TIME_STEP * inverse[None, :] * pair_push
            coords_now = coords_now + TIME_STEP * speed_now
        impulse = INNER * TIME_STEP * mass_here[None, :] * saxs_kick
        speed_now = speed_now.at[:, solute_slots].add(impulse)
    return (coords_now[None], speed_now[None])


def solution(mesh):
    in_specs = (
        P("rep", None, "sp"),
        P("rep", None, "sp"),
        P("rep", "sp"),
        P("rep", "sp"),
        P("rep", None, "sp", None),
        P("rep", "sp"),
        P("rep", "sp"),
        P(),
        P(),
    )
    out_specs = (P("rep", None, "sp"), P("rep", None, "sp"))
    return jax.shard_map(shards, mesh=mesh, in_specs=in_specs, out_specs=out_specs, check_vma=False)
```

profile of v0, /device:TPU:8, one launch (start us, length us, event | category | flops | bytes accessed | tf_op | source)
XLA Modules:
  0.0 896.0 jit_solution(11121404440708950667)
XLA Ops:
  7.3 3.4 copy.163
  10.7 2.9 copy.166
  13.6 3.5 collective-permute-start
  20.7 2.6 copy.164
  23.3 2.9 gather_fusion.4
  29.6 16.2 %while.84 = (s32[]{:T(128)}, f32[8,3,8,128]{3,2,1,0:T(8,128)S(1)}, f32[8,4,8,128]{3,2,0,1:T(8,128)S(1)}, f32[8,4,8,512]{3,2,0,1:T(8,128)S(1)}, s32[]{:T(128)}) while((s32[]{:T(128)}, f32[8,3,8,128]{3,2,1,0:T(8,128)S(1)}, f32[8,4,8,128]{3,2,0,1:T(8,128)S(1)}, f32[8,4,8,512]{3,2,0,1:T(8,128)S(1)}, s32[]{:T(128)}) %tuple.295), condition=%wide.region_4.6_spmd, body=%wide.region_0.5_spmd.sunk | while | flops 8916994 | bytes 446537 | solution.py:140
  45.9 2.7 copy.171
  48.5 7.0 multiply_add_fusion.6
  55.5 2.8 copy.172
  58.5 3.5 collective-permute-start.2
  62.0 2.9 collective-permute-start.3
  64.9 3.2 collective-permute-done.3
  69.8 16.2 %while.85 = (s32[]{:T(128)}, f32[8,3,8,128]{3,2,1,0:T(8,128)S(1)}, f32[8,4,8,128]{3,2,1,0:T(8,128)S(1)}, f32[8,4,8,512]{3,2,0,1:T(8,128)S(1)}, s32[]{:T(128)}, /*index=5*/s32[]{:T(128)}, s32[]{}, s32[]{}, s32[]{}) while((s32[]{:T(128)}, f32[8,3,8,128]{3,2,1,0:T(8,128)S(1)}, f32[8,4,8,128]{3,2,1,0:T(8,128)S(1)}, ...), condition=%wide.region_9.11_spmd, body=%wide.region_5.10_spmd.sunk | while | flops 8916997 | bytes 413849 | solution.py:140
  86.0 2.7 copy.178
  88.6 8.5 multiply_add_fusion.5
  97.2 2.9 gather_fusion.6
  100.1 2.8 copy.179
  103.7 150.7 %while.89 = (s32[]{:T(128)}, f32[6,2,8,784]{3,2,0,1:T(8,128)S(1)}, f32[1,256]{1,0:T(1,128)S(1)}, f32[6,8]{1,0:T(8,128)S(1)}, f32[256]{0:T(256)S(1)}, /*index=5*/...) while((s32[]{:T(128)}, f32[6,2,8,784]{3,2,0,1:T(8,128)S(1)}, ...), condition=%wide.region_37.40_spmd.clone, body=%wide.region_34.39_spmd.clone.sunk | while | flops 9031682 | bytes 1784213 | solution.py:69
  104.1 24.7 %fusion.158 = (f32[8,784]{1,0:T(8,128)S(1)}, f32[8,784]{1,0:T(8,128)S(1)}) fusion(f32[784,256]{1,0:T(8,128)S(1)} %multiply_add_fusion.13, f32[8]{0:T(128)S(1)} %fusion.157, f32[256]{0:T(256)S(1)} %bitcast.407), kind=kLoop, calls=%fused_computation.132.clone.1 | loop fusion | flops 8015616 | bytes 854048 | tf_op jit(solution)/shard_map/while/body/eval_jaxpr/reduce_sum | solution.py:64
  129.2 24.7 %fusion.158 = (f32[8,784]{1,0:T(8,128)S(1)}, f32[8,784]{1,0:T(8,128)S(1)}) fusion(f32[784,256]{1,0:T(8,128)S(1)} %multiply_add_fusion.13, f32[8]{0:T(128)S(1)} %fusion.157, f32[256]{0:T(256)S(1)} %bitcast.407), kind=kLoop, calls=%fused_computation.132.clone.1 | loop fusion | flops 8015616 | bytes 854048 | tf_op jit(solution)/shard_map/while/body/eval_jaxpr/reduce_sum | solution.py:64
  154.4 24.7 %fusion.158 = (f32[8,784]{1,0:T(8,128)S(1)}, f32[8,784]{1,0:T(8,128)S(1)}) fusion(f32[784,256]{1,0:T(8,128)S(1)} %multiply_add_fusion.13, f32[8]{0:T(128)S(1)} %fusion.157, f32[256]{0:T(256)S(1)} %bitcast.407), kind=kLoop, calls=%fused_computation.132.clone.1 | loop fusion | flops 8015616 | bytes 854048 | tf_op jit(solution)/shard_map/while/body/eval_jaxpr/reduce_sum | solution.py:64
  179.5 24.7 %fusion.158 = (f32[8,784]{1,0:T(8,128)S(1)}, f32[8,784]{1,0:T(8,128)S(1)}) fusion(f32[784,256]{1,0:T(8,128)S(1)} %multiply_add_fusion.13, f32[8]{0:T(128)S(1)} %fusion.157, f32[256]{0:T(256)S(1)} %bitcast.407), kind=kLoop, calls=%fused_computation.132.clone.1 | loop fusion | flops 8015616 | bytes 854048 | tf_op jit(solution)/shard_map/while/body/eval_jaxpr/reduce_sum | solution.py:64
  204.6 24.7 %fusion.158 = (f32[8,784]{1,0:T(8,128)S(1)}, f32[8,784]{1,0:T(8,128)S(1)}) fusion(f32[784,256]{1,0:T(8,128)S(1)} %multiply_add_fusion.13, f32[8]{0:T(128)S(1)} %fusion.157, f32[256]{0:T(256)S(1)} %bitcast.407), kind=kLoop, calls=%fused_computation.132.clone.1 | loop fusion | flops 8015616 | bytes 854048 | tf_op jit(solution)/shard_map/while/body/eval_jaxpr/reduce_sum | solution.py:64
  229.7 24.7 %fusion.158 = (f32[8,784]{1,0:T(8,128)S(1)}, f32[8,784]{1,0:T(8,128)S(1)}) fusion(f32[784,256]{1,0:T(8,128)S(1)} %multiply_add_fusion.13, f32[8]{0:T(128)S(1)} %fusion.157, f32[256]{0:T(256)S(1)} %bitcast.407), kind=kLoop, calls=%fused_computation.132.clone.1 | loop fusion | flops 8015616 | bytes 854048 | tf_op jit(solution)/shard_map/while/body/eval_jaxpr/reduce_sum | solution.py:64
  255.2 150.9 %while.88 = (s32[]{:T(128)}, f32[6,2,8,784]{3,2,0,1:T(8,128)S(1)}, f32[1,256]{1,0:T(1,128)S(1)}, f32[6,8]{1,0:T(8,128)S(1)}, f32[256]{0:T(256)S(1)}, /*index=5*/...) while((s32[]{:T(128)}, f32[6,2,8,784]{3,2,0,1:T(8,128)S(1)}, ...), condition=%wide.region_18.21_spmd.clone, body=%wide.region_15.20_spmd.clone.sunk | while | flops 9031682 | bytes 1784213 | solution.py:69
  255.8 24.7 %fusion.155 = (f32[8,784]{1,0:T(8,128)S(1)}, f32[8,784]{1,0:T(8,128)S(1)}) fusion(f32[784,256]{1,0:T(8,128)S(1)} %multiply_add_fusion.12, f32[8]{0:T(128)S(1)} %fusion.154, f32[256]{0:T(256)S(1)} %bitcast.408), kind=kLoop, calls=%fused_computation.121.clone.1 | loop fusion | flops 8015616 | bytes 854048 | tf_op jit(solution)/shard_map/while/body/eval_jaxpr/reduce_sum | solution.py:64
  280.9 24.7 %fusion.155 = (f32[8,784]{1,0:T(8,128)S(1)}, f32[8,784]{1,0:T(8,128)S(1)}) fusion(f32[784,256]{1,0:T(8,128)S(1)} %multiply_add_fusion.12, f32[8]{0:T(128)S(1)} %fusion.154, f32[256]{0:T(256)S(1)} %bitcast.408), kind=kLoop, calls=%fused_computation.121.clone.1 | loop fusion | flops 8015616 | bytes 854048 | tf_op jit(solution)/shard_map/while/body/eval_jaxpr/reduce_sum | solution.py:64
  306.0 24.7 %fusion.155 = (f32[8,784]{1,0:T(8,128)S(1)}, f32[8,784]{1,0:T(8,128)S(1)}) fusion(f32[784,256]{1,0:T(8,128)S(1)} %multiply_add_fusion.12, f32[8]{0:T(128)S(1)} %fusion.154, f32[256]{0:T(256)S(1)} %bitcast.408), kind=kLoop, calls=%fused_computation.121.clone.1 | loop fusion | flops 8015616 | bytes 854048 | tf_op jit(solution)/shard_map/while/body/eval_jaxpr/reduce_sum | solution.py:64
  331.1 24.7 %fusion.155 = (f32[8,784]{1,0:T(8,128)S(1)}, f32[8,784]{1,0:T(8,128)S(1)}) fusion(f32[784,256]{1,0:T(8,128)S(1)} %multiply_add_fusion.12, f32[8]{0:T(128)S(1)} %fusion.154, f32[256]{0:T(256)S(1)} %bitcast.408), kind=kLoop, calls=%fused_computation.121.clone.1 | loop fusion | flops 8015616 | bytes 854048 | tf_op jit(solution)/shard_map/while/body/eval_jaxpr/reduce_sum | solution.py:64
  356.3 24.7 %fusion.155 = (f32[8,784]{1,0:T(8,128)S(1)}, f32[8,784]{1,0:T(8,128)S(1)}) fusion(f32[784,256]{1,0:T(8,128)S(1)} %multiply_add_fusion.12, f32[8]{0:T(128)S(1)} %fusion.154, f32[256]{0:T(256)S(1)} %bitcast.408), kind=kLoop, calls=%fused_computation.121.clone.1 | loop fusion | flops 8015616 | bytes 854048 | tf_op jit(solution)/shard_map/while/body/eval_jaxpr/reduce_sum | solution.py:64
  381.4 24.7 %fusion.155 = (f32[8,784]{1,0:T(8,128)S(1)}, f32[8,784]{1,0:T(8,128)S(1)}) fusion(f32[784,256]{1,0:T(8,128)S(1)} %multiply_add_fusion.12, f32[8]{0:T(128)S(1)} %fusion.154, f32[256]{0:T(256)S(1)} %bitcast.408), kind=kLoop, calls=%fused_computation.121.clone.1 | loop fusion | flops 8015616 | bytes 854048 | tf_op jit(solution)/shard_map/while/body/eval_jaxpr/reduce_sum | solution.py:64
  406.8 4.8 collective-permute-start.4
  413.7 6.3 collective-permute-done.5
  421.6 16.2 %while.86 = (s32[]{:T(128)}, f32[8,3,8,128]{3,2,1,0:T(8,128)S(1)}, f32[8,4,8,128]{3,2,1,0:T(8,128)S(1)}, f32[8,4,8,512]{3,2,0,1:T(8,128)S(1)}, s32[]{:T(128)}, /*index=5*/s32[]{:T(128)}, s32[]{}, s32[]{}, s32[]{}) while((s32[]{:T(128)}, f32[8,3,8,128]{3,2,1,0:T(8,128)S(1)}, f32[8,4,8,128]{3,2,1,0:T(8,128)S(1)}, ...), condition=%wide.region_14.16_spmd, body=%wide.region_10.15_spmd.sunk | while | flops 8916997 | bytes 413849 | solution.py:140
  437.8 2.7 copy.185
  440.4 8.6 fusion.73
  449.1 43.6 %all-reduce.4.cloned.1.call-done = (f32[2,48,784]{2,1,0:T(8,128)}, f32[2,48,784]{2,1,0:T(8,128)}) async-done(((f32[2,48,784]{2,1,0:T(8,128)}, f32[2,48,784]{2,1,0:T(8,128)}), (f32[2,48,784]{2,1,0:T(8,128)}, f32[2,48,784]{2,1,0:T(8,128)})) %all-reduce.4.cloned.1.call-update) | async-done | bytes 602128 | tf_op jit(solution)/shard_map/psum | solution.py:173
  495.0 33.4 %all-reduce = (f32[48]{0:T(128)S(1)}, f32[48]{0:T(128)S(1)}) all-reduce(f32[48]{0:T(128)S(1)} %broadcast_multiply_fusion.5, f32[48]{0:T(128)S(1)} %broadcast_multiply_fusion.4), channel_id=1, replica_groups=mesh['rep'=16,'sp'=8] {'rep'}, use_global_device_ids=true, to_apply=%region_21.24 | all-reduce | flops 96 | bytes 768 | tf_op jit(solution)/shard_map/psum | solution.py:174
  529.5 146.9 %while.91 = (s32[]{:T(128)}, f32[784,256]{1,0:T(8,128)S(1)}, f32[6,8]{1,0:T(8,128)S(1)}, f32[6,8,784]{2,1,0:T(8,128)S(1)}, f32[6,8,784]{2,1,0:T(8,128)S(1)}, /*i...) while((s32[]{:T(128)}, f32[784,256]{1,0:T(8,128)S(1)}, ...), condition=%wide.region_43.46_spmd.clone, body=%wide.region_41.45_spmd.clone.sunk | while | flops 10838019 | bytes 4980143 | solution.py:97
  529.9 23.8 %fusion.163 = f32[784,256]{1,0:T(8,128)S(1)} fusion(f32[8,784]{1,0:T(8,128)S(1)} %get-tuple-element.1134, f32[784,256]{1,0:T(8,128)S(1)} %multiply_add_fusion.15, f32[8,784]{1,0:T(8,128)S(1)} %get-tuple-element.1135, f32[8]{0:T(128)S(1)} %fusion.162), kind=kLoop, calls=%fused_computation.158.clone.1 | loop fusion | flops 9433088 | bytes 1655840 | tf_op jit(solution)/shard_map/while/body/eval_jaxpr/reduce_sum | solution.py:90
  554.4 23.8 %fusion.163 = f32[784,256]{1,0:T(8,128)S(1)} fusion(f32[8,784]{1,0:T(8,128)S(1)} %get-tuple-element.1134, f32[784,256]{1,0:T(8,128)S(1)} %multiply_add_fusion.15, f32[8,784]{1,0:T(8,128)S(1)} %get-tuple-element.1135, f32[8]{0:T(128)S(1)} %fusion.162), kind=kLoop, calls=%fused_computation.158.clone.1 | loop fusion | flops 9433088 | bytes 1655840 | tf_op jit(solution)/shard_map/while/body/eval_jaxpr/reduce_sum | solution.py:90
  578.9 23.8 %fusion.163 = f32[784,256]{1,0:T(8,128)S(1)} fusion(f32[8,784]{1,0:T(8,128)S(1)} %get-tuple-element.1134, f32[784,256]{1,0:T(8,128)S(1)} %multiply_add_fusion.15, f32[8,784]{1,0:T(8,128)S(1)} %get-tuple-element.1135, f32[8]{0:T(128)S(1)} %fusion.162), kind=kLoop, calls=%fused_computation.158.clone.1 | loop fusion | flops 9433088 | bytes 1655840 | tf_op jit(solution)/shard_map/while/body/eval_jaxpr/reduce_sum | solution.py:90
  603.3 23.8 %fusion.163 = f32[784,256]{1,0:T(8,128)S(1)} fusion(f32[8,784]{1,0:T(8,128)S(1)} %get-tuple-element.1134, f32[784,256]{1,0:T(8,128)S(1)} %multiply_add_fusion.15, f32[8,784]{1,0:T(8,128)S(1)} %get-tuple-element.1135, f32[8]{0:T(128)S(1)} %fusion.162), kind=kLoop, calls=%fused_computation.158.clone.1 | loop fusion | flops 9433088 | bytes 1655840 | tf_op jit(solution)/shard_map/while/body/eval_jaxpr/reduce_sum | solution.py:90
  627.8 23.8 %fusion.163 = f32[784,256]{1,0:T(8,128)S(1)} fusion(f32[8,784]{1,0:T(8,128)S(1)} %get-tuple-element.1134, f32[784,256]{1,0:T(8,128)S(1)} %multiply_add_fusion.15, f32[8,784]{1,0:T(8,128)S(1)} %get-tuple-element.1135, f32[8]{0:T(128)S(1)} %fusion.162), kind=kLoop, calls=%fused_computation.158.clone.1 | loop fusion | flops 9433088 | bytes 1655840 | tf_op jit(solution)/shard_map/while/body/eval_jaxpr/reduce_sum | solution.py:90
  652.3 23.8 %fusion.163 = f32[784,256]{1,0:T(8,128)S(1)} fusion(f32[8,784]{1,0:T(8,128)S(1)} %get-tuple-element.1134, f32[784,256]{1,0:T(8,128)S(1)} %multiply_add_fusion.15, f32[8,784]{1,0:T(8,128)S(1)} %get-tuple-element.1135, f32[8]{0:T(128)S(1)} %fusion.162), kind=kLoop, calls=%fused_computation.158.clone.1 | loop fusion | flops 9433088 | bytes 1655840 | tf_op jit(solution)/shard_map/while/body/eval_jaxpr/reduce_sum | solution.py:90
  676.5 146.9 %while.90 = (s32[]{:T(128)}, f32[784,256]{1,0:T(8,128)S(1)}, f32[6,8]{1,0:T(8,128)S(1)}, f32[6,8,784]{2,1,0:T(8,128)S(1)}, f32[6,8,784]{2,1,0:T(8,128)S(1)}, /*i...) while((s32[]{:T(128)}, f32[784,256]{1,0:T(8,128)S(1)}, ...), condition=%wide.region_24.27_spmd.clone, body=%wide.region_22.26_spmd.clone.sunk | while | flops 10838019 | bytes 4980143 | solution.py:97
  676.9 23.8 %fusion.161 = f32[784,256]{1,0:T(8,128)S(1)} fusion(f32[8,784]{1,0:T(8,128)S(1)} %get-tuple-element.1121, f32[784,256]{1,0:T(8,128)S(1)} %multiply_add_fusion.14, f32[8,784]{1,0:T(8,128)S(1)} %get-tuple-element.1122, f32[8]{0:T(128)S(1)} %fusion.160), kind=kLoop, calls=%fused_computation.145.clone.1 | loop fusion | flops 9433088 | bytes 1655840 | tf_op jit(solution)/shard_map/while/body/eval_jaxpr/reduce_sum | solution.py:90
  701.4 23.8 %fusion.161 = f32[784,256]{1,0:T(8,128)S(1)} fusion(f32[8,784]{1,0:T(8,128)S(1)} %get-tuple-element.1121, f32[784,256]{1,0:T(8,128)S(1)} %multiply_add_fusion.14, f32[8,784]{1,0:T(8,128)S(1)} %get-tuple-element.1122, f32[8]{0:T(128)S(1)} %fusion.160), kind=kLoop, calls=%fused_computation.145.clone.1 | loop fusion | flops 9433088 | bytes 1655840 | tf_op jit(solution)/shard_map/while/body/eval_jaxpr/reduce_sum | solution.py:90
  725.9 23.8 %fusion.161 = f32[784,256]{1,0:T(8,128)S(1)} fusion(f32[8,784]{1,0:T(8,128)S(1)} %get-tuple-element.1121, f32[784,256]{1,0:T(8,128)S(1)} %multiply_add_fusion.14, f32[8,784]{1,0:T(8,128)S(1)} %get-tuple-element.1122, f32[8]{0:T(128)S(1)} %fusion.160), kind=kLoop, calls=%fused_computation.145.clone.1 | loop fusion | flops 9433088 | bytes 1655840 | tf_op jit(solution)/shard_map/while/body/eval_jaxpr/reduce_sum | solution.py:90
  750.4 23.8 %fusion.161 = f32[784,256]{1,0:T(8,128)S(1)} fusion(f32[8,784]{1,0:T(8,128)S(1)} %get-tuple-element.1121, f32[784,256]{1,0:T(8,128)S(1)} %multiply_add_fusion.14, f32[8,784]{1,0:T(8,128)S(1)} %get-tuple-element.1122, f32[8]{0:T(128)S(1)} %fusion.160), kind=kLoop, calls=%fused_computation.145.clone.1 | loop fusion | flops 9433088 | bytes 1655840 | tf_op jit(solution)/shard_map/while/body/eval_jaxpr/reduce_sum | solution.py:90
  774.8 23.8 %fusion.161 = f32[784,256]{1,0:T(8,128)S(1)} fusion(f32[8,784]{1,0:T(8,128)S(1)} %get-tuple-element.1121, f32[784,256]{1,0:T(8,128)S(1)} %multiply_add_fusion.14, f32[8,784]{1,0:T(8,128)S(1)} %get-tuple-element.1122, f32[8]{0:T(128)S(1)} %fusion.160), kind=kLoop, calls=%fused_computation.145.clone.1 | loop fusion | flops 9433088 | bytes 1655840 | tf_op jit(solution)/shard_map/while/body/eval_jaxpr/reduce_sum | solution.py:90
  799.3 23.8 %fusion.161 = f32[784,256]{1,0:T(8,128)S(1)} fusion(f32[8,784]{1,0:T(8,128)S(1)} %get-tuple-element.1121, f32[784,256]{1,0:T(8,128)S(1)} %multiply_add_fusion.14, f32[8,784]{1,0:T(8,128)S(1)} %get-tuple-element.1122, f32[8]{0:T(128)S(1)} %fusion.160), kind=kLoop, calls=%fused_computation.145.clone.1 | loop fusion | flops 9433088 | bytes 1655840 | tf_op jit(solution)/shard_map/while/body/eval_jaxpr/reduce_sum | solution.py:90
  823.9 5.9 scatter_fusion
  829.9 5.9 multiply_add_fusion.4
  835.7 2.8 copy.188
  838.7 3.1 collective-permute-start.6
  841.8 3.0 collective-permute-start.7
  845.0 3.0 collective-permute-done.7
  849.6 16.2 %while.87 = (s32[]{:T(128)}, f32[8,3,8,128]{3,2,1,0:T(8,128)S(1)}, f32[8,4,8,128]{3,2,1,0:T(8,128)S(1)}, f32[8,4,8,512]{3,2,0,1:T(8,128)S(1)}, s32[]{:T(128)}, /*index=5*/s32[]{:T(128)}, s32[]{}, s32[]{}, s32[]{}) while((s32[]{:T(128)}, f32[8,3,8,128]{3,2,1,0:T(8,128)S(1)}, f32[8,4,8,128]{3,2,1,0:T(8,128)S(1)}, ...), condition=%wide.region_33.36_spmd, body=%wide.region_29.35_spmd.sunk | while | flops 8916997 | bytes 413849 | solution.py:140
  865.8 2.7 copy.193
  868.5 7.7 add_bitcast_fusion
  876.1 5.9 scatter_fusion.1
  882.0 3.5 copy.197
  885.5 3.5 copy.196
  (370 shorter events, 95.4 us)
Async XLA Ops:
  7.2 6.4 copy-start.1
  7.2 12.3 %copy-start.5 = (s32[1,4,64,4]{2,3,1,0:T(4,128)S(1)}, s32[1,4,64,4]{2,3,1,0:T(4,128)}, u32[]{:S(2)}) copy-start(s32[1,4,64,4]{2,3,1,0:T(4,128)} %param.33) | copy-start | bytes 12292
  7.2 12.8 %copy-start.6 = (s32[1,256]{1,0:T(1,128)S(1)}, s32[1,256]{1,0:T(1,128)}, u32[]{:S(2)}) copy-start(s32[1,256]{1,0:T(1,128)} %param.34) | copy-start | bytes 3076
  7.2 13.4 %copy-start = (f32[1,8192]{1,0:T(1,128)S(1)}, f32[1,8192]{1,0:T(1,128)}, u32[]{:S(2)}) copy-start(f32[1,8192]{1,0:T(1,128)} %param.32) | copy-start | bytes 98308
  7.2 13.5 %copy-start.4 = (f32[1,3,8192]{2,0,1:T(1,128)S(1)}, f32[1,3,8192]{2,0,1:T(1,128)}, u32[]{:S(2)}) copy-start(f32[1,3,8192]{2,0,1:T(1,128)} %param.30) | copy-start | bytes 294916
  7.2 485.5 %all-reduce.4.cloned.1.call-start = ((), (), s32[]{:S(2)}) async-start(), calls=%async_computation | async-start | bytes 1376256 | tf_op jit(solution)/shard_map/psum | solution.py:173
  10.7 17.3 %copy-start.3 = (f32[1,3,8192]{2,0,1:T(1,128)S(1)}, f32[1,3,8192]{2,0,1:T(1,128)}, u32[]{:S(2)}) copy-start(f32[1,3,8192]{2,0,1:T(1,128)} %param.29) | copy-start | bytes 294916
  13.6 14.4 %collective-permute-start = (f32[4,4096]{1,0:T(4,128)S(1)}, f32[4,4096]{1,0:T(4,128)S(1)}, u32[]{:S(2)}, u32[]{:S(2)}) collective-permute-start(f32[4,4096]{1,0:T(4,128)S(1)} %get-tuple-element.653), channel_id=1, source_target_pairs={{0,1},{1,2},{2,3},{3,4},{4,5},{5,6},{6,7},{8,9},{9,10},{10,11},{11... | collective-permute-start | bytes 196616 | tf_op jit(solution)/shard_map/ppermute | solution.py:28
  17.1 10.9 %collective-permute-start.1 = (f32[4,4096]{1,0:T(4,128)S(1)}, f32[4,4096]{1,0:T(4,128)S(1)}, u32[]{:S(2)}, u32[]{:S(2)}) collective-permute-start(f32[4,4096]{1,0:T(4,128)S(1)} %get-tuple-element.654), channel_id=1, source_target_pairs={{1,0},{2,1},{3,2},{4,3},{5,4},{6,5},{7,6},{9,8},{10,9},{11,10},{12... | collective-permute-start | bytes 196616 | tf_op jit(solution)/shard_map/ppermute | solution.py:30
  58.5 6.4 collective-permute-start.2
  62.0 6.2 collective-permute-start.3
  97.2 6.5 copy-start.7
  406.8 6.8 collective-permute-start.4
  411.7 8.3 collective-permute-start.5
  440.4 87.9 %copy-start.8 = (f32[48]{0:T(128)S(1)}, f32[48]{0:T(128)}, u32[]{:S(2)}) copy-start(f32[48]{0:T(128)} %param.36) | copy-start | bytes 580
  440.4 87.9 %copy-start.9 = (f32[48]{0:T(128)S(1)}, f32[48]{0:T(128)}, u32[]{:S(2)}) copy-start(f32[48]{0:T(128)} %param.37) | copy-start | bytes 580
  529.5 146.9 %copy-start.2 = (f32[2,48,784]{2,1,0:T(8,128)S(1)}, f32[2,48,784]{2,1,0:T(8,128)}, u32[]{:S(2)}) copy-start(f32[2,48,784]{2,1,0:T(8,128)} %get-tuple-element.603) | copy-start | bytes 903172
  838.7 6.3 collective-permute-start.6
  841.8 6.2 collective-permute-start.7
Sparse Core Ops, SparseCore 0:
  413.8 78.8 all-reduce.3
where the time goes:
time: 904 us; the launch traced here: 896 us
  other arithmetic  713 us (79%)
  waiting for transfers between devices  56.1 us (6%)
  local copies, waits for them, and re-layouts  49.9 us (6%)
  blocking collectives  33.4 us (4%)
  starting transfers between devices  25.1 us (3%)
  between operations  15.1 us (2%)
    reduce_sum x12, other arithmetic, one_block(): jnp.sum(weights * jnp.cos(phases), axis=-1)  296 us
    reduce_sum x12, other arithmetic, add_block(): jnp.sum(shell_block[:, None, None] * (block_imag[:, :, None] * jnp.cos(ph...  286 us
    reduce_sum x32, other arithmetic, pair_group(): jnp.sum(pair_weight * delta, axis=-1)  61.6 us
    psum x1, waiting for transfers between devices, shards(): amplitude = lax.psum(partial_value, 'sp')  43.6 us
    psum x1, blocking collectives, shards(): intensity = lax.psum(shell_intensity(amplitude), 'rep') / replica_count  33.4 us
    add x3, other arithmetic, shards(): coords_now = coords_now + TIME_STEP * speed_now  21.4 us
  transfers between devices with their start and end apart: 9, of which 4 were waited for; matrix products, arithmetic and copies ran while one was open for 4% of the time, Pallas kernels for 0%

commit v1 on v0

v1 whole, which is shorter than its diff:
```python
import functools
import math

import jax
import jax.numpy as jnp
import numpy as np
from jax import lax
from jax.experimental import pallas as pl
from jax.experimental.pallas import tpu as pltpu
from jax.sharding import PartitionSpec as P

M = 784
NQ = 48
OUTER = 2
INNER = 2
TIME_STEP = 0.05
PAIR_STRENGTH = 0.2
HALF_INVERSE = 0.03125

BLOCK = 128
NB = 64
HB = 32
EXT = NB + 2 * HB
NEIGHBOURS = 4
ATOMS = NB * BLOCK
HALO = HB * BLOCK
SOL = 256
PARTS = 8
REPLICAS = 16
DIR_PART = M // PARTS
GROUPS = -(-DIR_PART // 8)
CENTERS = NQ // 3
LANE_GROUPS = PARTS * SOL // 128
CHUNK = 4
FILL_UNROLL = 16
BLOCK_UNROLL = 16

ALPHA = math.sqrt(HALF_INVERSE * math.log2(math.e))
COUPLING = PAIR_STRENGTH / math.sqrt(NEIGHBOURS * BLOCK)
NORM = 1.0 / math.sqrt(PARTS * SOL)
TURN = 1.0 / (32.0 * math.pi)

F32 = jnp.float32
BF16 = jnp.bfloat16


def direction_table():
    order = np.arange(M)
    height = 1.0 - (2.0 * order + 1.0) / M
    radius = np.sqrt(1.0 - height * height)
    azimuth = (order * 610 % 987) * (2.0 * math.pi / 987.0)
    rows = np.stack([radius * np.cos(azimuth), radius * np.sin(azimuth), height], axis=-1) * TURN
    table = np.zeros((PARTS, GROUPS * 8, 3), np.float32)
    table[:, :DIR_PART] = rows.reshape(PARTS, DIR_PART, 3)
    return table


def split3(value):
    high = value.astype(BF16).astype(F32)
    rest = value - high
    mid = rest.astype(BF16).astype(F32)
    return high, mid, rest - mid


def rows_of(shape):
    return lax.broadcasted_iota(jnp.int32, shape, 0)


def neighbour_features(cell):
    row = rows_of((8, BLOCK))
    both = jnp.concatenate([cell, cell], axis=0)
    charge = jnp.broadcast_to(cell[3:4], (8, BLOCK))
    moments = jnp.where((row & 3) == 3, charge, both * charge)
    th, tm, tl = split3(moments)
    weights = jnp.concatenate([jnp.where(row < 4, th, tm), jnp.where(row < 4, tl, 0.0)], axis=0)
    scaled = both * ALPHA
    space = row < 3
    norm = -jnp.sum(jnp.where(space, scaled * scaled, 0.0), axis=0, keepdims=True)
    h, m, l = split3(jnp.where(space, scaled, jnp.where(row == 4, norm, 0.0)))
    one = jnp.where(row == 3, 1.0, 0.0)
    mh = jnp.where(space, h, 0.0)
    near = jnp.concatenate([h + one, m + one, l + one, mh, jnp.where(space, m, 0.0), mh], axis=0)
    return near.astype(BF16), weights.astype(BF16)


def own_features(cell):
    row = rows_of((8, BLOCK))
    both = jnp.concatenate([cell, cell], axis=0)
    scaled = both * ALPHA
    space = row < 3
    norm = -jnp.sum(jnp.where(space, scaled * scaled, 0.0), axis=0, keepdims=True)
    h, m, l = split3(jnp.where(space, 2.0 * scaled, jnp.where(row == 3, norm, 0.0)))
    one = jnp.where(row == 4, 1.0, 0.0)
    mo = jnp.where(space, m, 0.0)
    own = jnp.concatenate(
        [h + one, jnp.where(space, h, m) + one, jnp.where(space, h, l) + one, mo, mo, jnp.where(space, l, 0.0)],
        axis=0,
    )
    return own.astype(BF16)


def selectors(index):
    block = lax.shift_right_logical(index, 7)
    lane = index & 127
    by_block = rows_of((NB, SOL)) == block
    by_lane = rows_of((BLOCK, SOL)) == lane
    return by_block, by_lane


def scatter_kicks(index_ref, weight_ref, kick_ref, push_ref):
    by_block, by_lane = selectors(index_ref[...])
    total = kick_ref[0]
    for part in range(1, PARTS):
        total = total + kick_ref[part]
    total = total * (weight_ref[...] * (-INNER * TIME_STEP))
    lanes = jnp.where(by_lane, 1.0, 0.0).astype(BF16)
    lanes = jnp.concatenate([lanes, lanes, lanes], axis=1)
    for c in range(3):
        parts = split3(total[c : c + 1])
        rows = jnp.concatenate([jnp.where(by_block, p, 0.0).astype(BF16) for p in parts], axis=1)
        push_ref[c] = lax.dot_general(rows, lanes, (((1,), (1,)), ((), ())), preferred_element_type=F32)


def gather_points(index_ref, weight_ref, place_ref, point_ref):
    by_block, by_lane = selectors(index_ref[...])
    lanes = jnp.where(by_lane, 1.0, 0.0).astype(BF16)
    found = []
    for c in range(3):
        total = None
        for p in split3(place_ref[c]):
            part = jnp.dot(p.astype(BF16), lanes, preferred_element_type=F32)
            total = part if total is None else total + part
        found.append(jnp.sum(jnp.where(by_block, total, 0.0), axis=0, keepdims=True))
    found.append(weight_ref[...])
    points = jnp.concatenate(found, axis=0)
    for part in range(PARTS):
        point_ref[part] = points


def block_at(b):
    return pl.ds(pl.multiple_of(b * BLOCK, BLOCK), BLOCK)


def pushed(push_ref, b):
    return jnp.concatenate([push_ref[c, pl.ds(b, 1), :] for c in range(3)], axis=0)


def pack_kernel(pos_ref, charge_ref, vel_ref, inverse_ref, index_ref, weight_ref, *refs):
    out_ref, head_ref, tail_ref, point_ref, place_ref = refs

    def one_block(b, carry):
        at = block_at(b)
        place = pos_ref[:, at]
        out_ref[:, at] = jnp.concatenate([place, charge_ref[:, at], vel_ref[:, at], inverse_ref[:, at]], axis=0)
        for c in range(3):
            place_ref[c, pl.ds(b, 1), :] = place[c : c + 1]
        return carry

    lax.fori_loop(0, NB, one_block, 0, unroll=FILL_UNROLL)
    head_ref[...] = out_ref[0:4, 0:HALO]
    tail_ref[...] = out_ref[0:4, HALO:ATOMS]
    gather_points(index_ref, weight_ref, place_ref, point_ref)


def finish_kernel(vel_ref, inverse_ref, index_ref, weight_ref, kick_ref, out_ref, push_ref):
    scatter_kicks(index_ref, weight_ref, kick_ref, push_ref)

    def one_block(b, carry):
        at = block_at(b)
        out_ref[:, at] = vel_ref[:, at] + inverse_ref[:, at] * pushed(push_ref, b)
        return carry

    lax.fori_loop(0, NB, one_block, 0, unroll=FILL_UNROLL)


def pair_kernel(step, kicked, gathers, last, *refs):
    refs = list(refs)
    tile_ref, position_ref, state_ref, left_ref, right_ref = refs[:5]
    refs = refs[5:]
    if kicked or gathers:
        index_ref, weight_ref = refs[:2]
        refs = refs[2:]
    if kicked:
        kick_ref = refs.pop(0)
    if last:
        pos_ref, vel_ref = refs[:2]
        refs = refs[2:]
    else:
        out_ref, head_ref, tail_ref = refs[:3]
        refs = refs[3:]
    if gathers:
        point_ref = refs.pop(0)
    near_ref, moment_ref, own_ref = refs[:3]
    refs = refs[3:]
    if gathers:
        place_ref = refs.pop(0)
    if kicked:
        push_ref = refs.pop(0)

    left_ok = jnp.where(position_ref[0] > 0, 1.0, 0.0)
    right_ok = jnp.where(position_ref[0] < PARTS - 1, 1.0, 0.0)
    row4 = rows_of((4, BLOCK))

    def fill(slot, cell):
        near, moments = neighbour_features(cell)
        near_ref[slot] = near.T
        moment_ref[slot] = moments

    def fill_halo(b, carry):
        at = block_at(b)
        fill(b, left_ref[:, at] * jnp.where(row4 == 3, left_ok, 1.0))
        fill(b + HB + NB, right_ref[:, at] * jnp.where(row4 == 3, right_ok, 1.0))
        return carry

    lax.fori_loop(0, HB, fill_halo, 0, unroll=FILL_UNROLL)

    def fill_own(b, carry):
        cell = state_ref[0:4, block_at(b)]
        fill(b + HB, cell)
        own_ref[b] = own_features(cell)
        return carry

    lax.fori_loop(0, NB, fill_own, 0, unroll=FILL_UNROLL)

    if kicked:
        scatter_kicks(index_ref, weight_ref, kick_ref, push_ref)

    def one_block(b, carry):
        entries = [tile_ref[step * NB * NEIGHBOURS + b * NEIGHBOURS + i] for i in range(NEIGHBOURS)]
        near = jnp.concatenate([near_ref[e] for e in entries], axis=0)
        moments = jnp.concatenate([moment_ref[e] for e in entries], axis=1)
        weight = jnp.exp2(jnp.dot(near, own_ref[b], preferred_element_type=F32))
        high = weight.astype(BF16)
        low = (weight - high.astype(F32)).astype(BF16)
        sums = jnp.dot(moments, high, preferred_element_type=F32)
        sums = sums + jnp.dot(moments, low, preferred_element_type=F32)
        sums = sums[0:4] + sums[4:8] + sums[8:12]
        at = block_at(b)
        cell = state_ref[:, at]
        place, charge, speed, inverse = cell[0:3], cell[3:4], cell[4:7], cell[7:8]
        force = (COUPLING * charge) * (place * sums[3:4] - sums[0:3])
        if kicked:
            speed = speed + inverse * pushed(push_ref, b)
        speed = speed + (TIME_STEP * inverse) * force
        place = place + TIME_STEP * speed
        if gathers:
            for c in range(3):
                place_ref[c, pl.ds(b, 1), :] = place[c : c + 1]
        if last:
            pos_ref[:, at] = place
            vel_ref[:, at] = speed
        else:
            out_ref[:, at] = jnp.concatenate([place, charge, speed, inverse], axis=0)
        return carry

    lax.fori_loop(0, NB, one_block, 0, unroll=BLOCK_UNROLL)

    if not last:
        head_ref[...] = out_ref[0:4, 0:HALO]
        tail_ref[...] = out_ref[0:4, HALO:ATOMS]
    if gathers:
        gather_points(index_ref, weight_ref, place_ref, point_ref)


VMEM = pl.BlockSpec(memory_space=pltpu.VMEM)
SMEM = pl.BlockSpec(memory_space=pltpu.SMEM)
PARAMS = pltpu.CompilerParams(vmem_limit_bytes=32 << 20)


def pack(positions, strength, velocities, inv_mass, index, weights):
    return pl.pallas_call(
        pack_kernel,
        out_shape=[
            jax.ShapeDtypeStruct((8, ATOMS), F32),
            jax.ShapeDtypeStruct((4, HALO), F32),
            jax.ShapeDtypeStruct((4, HALO), F32),
            jax.ShapeDtypeStruct((PARTS, 4, SOL), F32),
        ],
        in_specs=[VMEM] * 6,
        out_specs=[VMEM] * 4,
        scratch_shapes=[pltpu.VMEM((3, NB, BLOCK), F32)],
        compiler_params=PARAMS,
        cost_estimate=pl.CostEstimate(flops=100_000_000, bytes_accessed=600_000, transcendentals=0),
        name="pack",
    )(positions, strength, velocities, inv_mass, index, weights)


def finish(velocities, inv_mass, index, weights, kick):
    return pl.pallas_call(
        finish_kernel,
        out_shape=jax.ShapeDtypeStruct((3, ATOMS), F32),
        in_specs=[VMEM] * 5,
        out_specs=VMEM,
        scratch_shapes=[pltpu.VMEM((3, NB, BLOCK), F32)],
        compiler_params=PARAMS,
        cost_estimate=pl.CostEstimate(flops=100_000_000, bytes_accessed=300_000, transcendentals=0),
        name="finish",
    )(velocities, inv_mass, index, weights, kick)


def pair_step(step, tiles, position, state, halo, index=None, weights=None, kick=None, gathers=False, last=False):
    kicked = kick is not None
    operands = [tiles, position, state, halo[0], halo[1]]
    specs = [SMEM, SMEM, VMEM, VMEM, VMEM]
    if kicked or gathers:
        operands += [index, weights]
        specs += [VMEM, VMEM]
    if kicked:
        operands.append(kick)
        specs.append(VMEM)
    scratch = [
        pltpu.VMEM((EXT, BLOCK, 48), BF16),
        pltpu.VMEM((EXT, 16, BLOCK), BF16),
        pltpu.VMEM((NB, 48, BLOCK), BF16),
    ]
    if last:
        shapes = [jax.ShapeDtypeStruct((3, ATOMS), F32)] * 2
    else:
        shapes = [jax.ShapeDtypeStruct((8, ATOMS), F32)] + [jax.ShapeDtypeStruct((4, HALO), F32)] * 2
    if gathers:
        shapes.append(jax.ShapeDtypeStruct((PARTS, 4, SOL), F32))
        scratch.append(pltpu.VMEM((3, NB, BLOCK), F32))
    if kicked:
        scratch.append(pltpu.VMEM((3, NB, BLOCK), F32))
    return pl.pallas_call(
        functools.partial(pair_kernel, step, kicked, gathers, last),
        out_shape=shapes,
        in_specs=specs,
        out_specs=[VMEM] * len(shapes),
        scratch_shapes=scratch,
        compiler_params=PARAMS,
        cost_estimate=pl.CostEstimate(flops=6_000_000_000, bytes_accessed=2_000_000, transcendentals=4_000_000),
        name="pair_step",
    )(*operands)


def double(cos, sin):
    twice = sin + sin
    return 1.0 - twice * sin, twice * cos


def product(a, b):
    return a[0] * b[0] - a[1] * b[1], a[1] * b[0] + a[0] * b[1]


def product_conj(a, b):
    return a[0] * b[0] + a[1] * b[1], a[1] * b[0] - a[0] * b[1]


def unit_powers(turns):
    y = (turns - jnp.round(turns)) * (0.5 * math.pi)
    z = y * y
    sin = ((-1.9515295891e-4 * z + 8.3321608736e-3) * z - 1.6666654611e-1) * (z * y) + y
    cos = ((2.443315711809948e-5 * z - 1.388731625493765e-3) * z + 4.166664568298827e-2) * (z * z) + (1.0 - 0.5 * z)
    one = double(*double(cos, sin))
    two = double(*one)
    three = product(two, one)
    sixteen = double(*double(*double(*two)))
    return one, three, product(sixteen, one)


def group_turns(dir_ref, point_ref, part, half):
    lanes = slice(half * 128, half * 128 + 128)

    def coordinate(c):
        return jnp.broadcast_to(point_ref[part, c : c + 1, lanes], (8, 128))

    u = [jnp.broadcast_to(dir_ref[0, :, c : c + 1], (8, 128)) for c in range(3)]
    return u[0] * coordinate(0) + u[1] * coordinate(1) + u[2] * coordinate(2), coordinate(3)


def amplitude_kernel(position_ref, point_ref, dir_ref, amp_ref, inten_ref, acc_ref, square_ref):
    group = pl.program_id(0)
    zero = jnp.zeros((8, 128), F32)

    @pl.when(group == 0)
    def _():
        square_ref[...] = zero

    for i in range(6 * CENTERS):
        acc_ref[i] = zero

    def chunk(at, carry):
        state = []
        for n in range(CHUNK):
            turns, weight = group_turns(dir_ref, point_ref, at * (CHUNK // 2) + n // 2, n % 2)
            one, three, start = unit_powers(turns)
            now = (weight * start[0], weight * start[1])
            before = product_conj(now, three)
            state.append([one[0], one[1], three[0] + three[0], now[0], now[1], before[0], before[1]])
        for k in range(CENTERS):
            sums = None
            for n in range(CHUNK):
                c1, s1, step, c, s, cb, sb = state[n]
                terms = [c, s, c * c1, s * s1, s * c1, c * s1]
                sums = terms if sums is None else [p + q for p, q in zip(sums, terms)]
                if k + 1 < CENTERS:
                    state[n][3:] = [step * c - cb, step * s - sb, c, s]
            for i in range(6):
                acc_ref[6 * k + i] += sums[i]
        return carry

    lax.fori_loop(0, LANE_GROUPS // CHUNK, chunk, 0, unroll=True)

    lane = lax.broadcasted_iota(jnp.int32, (8, 128), 1)
    inside = rows_of((8, 128)) + group * 8 < DIR_PART
    real = zero
    imag = zero
    for k in range(CENTERS):
        c, s, t1, t2, t3, t4 = [acc_ref[6 * k + i] for i in range(6)]
        for i, (a, b) in enumerate([(t1 + t2, t3 - t4), (c, s), (t1 - t2, t3 + t4)]):
            here = lane == 16 * i + k
            real = jnp.where(here, jnp.sum(a, axis=1, keepdims=True), real)
            imag = jnp.where(here, jnp.sum(b, axis=1, keepdims=True), imag)
    real = real * NORM
    imag = imag * NORM
    amp_ref[0, 0] = real
    amp_ref[0, 1] = imag
    square_ref[...] += jnp.where(inside, real * real + imag * imag, 0.0)

    @pl.when(group == GROUPS - 1)
    def _():
        inten_ref[...] = jnp.broadcast_to(jnp.sum(square_ref[...], axis=0, keepdims=True), inten_ref.shape)


def point_spec():
    return pl.BlockSpec((PARTS, 4, SOL), lambda g, p: (0, 0, 0))


def direction_spec():
    return pl.BlockSpec((1, 8, 3), lambda g, p: (p[0], g, 0))


def amplitudes(position, points, directions):
    return pl.pallas_call(
        amplitude_kernel,
        grid_spec=pltpu.PrefetchScalarGridSpec(
            num_scalar_prefetch=1,
            grid=(GROUPS,),
            in_specs=[point_spec(), direction_spec()],
            out_specs=[
                pl.BlockSpec((1, 2, 8, 128), lambda g, p: (g, 0, 0, 0)),
                pl.BlockSpec((PARTS * REPLICAS, 128), lambda g, p: (0, 0)),
            ],
            scratch_shapes=[pltpu.VMEM((6 * CENTERS, 8, 128), F32), pltpu.VMEM((8, 128), F32)],
        ),
        out_shape=[
            jax.ShapeDtypeStruct((GROUPS, 2, 8, 128), F32),
            jax.ShapeDtypeStruct((PARTS * REPLICAS, 128), F32),
        ],
        compiler_params=PARAMS,
        cost_estimate=pl.CostEstimate(flops=10_000_000_000, bytes_accessed=1_000_000, transcendentals=0),
        name="amplitudes",
    )(position, points, directions)


def kick_kernel(position_ref, point_ref, dir_ref, amp_ref, inten_ref, shell_ref, out_ref, coef_ref, scale_ref, acc_ref):
    group = pl.program_id(0)

    @pl.when(group == 0)
    def _():
        intensity = jnp.sum(inten_ref[...], axis=0, keepdims=True) * (1.0 / (M * REPLICAS))
        lane = lax.broadcasted_iota(jnp.int32, (1, 128), 1)
        shell = 1.0 + (3 * (lane & 15) + lax.shift_right_logical(lane, 4)).astype(F32) * (3.0 / NQ)
        factor = shell_ref[0:1] * (intensity - shell_ref[1:2]) * (2.0 / M) * shell
        scale_ref[...] = jnp.broadcast_to(factor, (8, 128))
        for i in range(LANE_GROUPS * 3):
            acc_ref[i] = jnp.zeros((8, 128), F32)

    b = amp_ref[0, 0] * scale_ref[...]
    a = amp_ref[0, 1] * scale_ref[...]
    for k in range(CENTERS):
        ax = [jnp.broadcast_to(a[:, 16 * i + k : 16 * i + k + 1], (8, 128)) for i in range(3)]
        bx = [jnp.broadcast_to(b[:, 16 * i + k : 16 * i + k + 1], (8, 128)) for i in range(3)]
        for i, v in enumerate([ax[1], ax[0] + ax[2], bx[0] - bx[2], bx[1], bx[0] + bx[2], ax[2] - ax[0]]):
            coef_ref[6 * k + i] = v

    def chunk(at, carry):
        state = []
        for n in range(CHUNK):
            turns, _ = group_turns(dir_ref, point_ref, at * (CHUNK // 2) + n // 2, n % 2)
            one, three, start = unit_powers(turns)
            state.append([one, three, start, three[0] + three[0], None, None, None, None])
        for k in range(CENTERS - 1, -1, -1):
            a1, ap, bm, b1, bp, am = [coef_ref[6 * k + i] for i in range(6)]
            for n in range(CHUNK):
                one, three, start, step, r1, i1, r2, i2 = state[n]
                real = a1 + ap * one[0] + bm * one[1]
                imag = b1 + bp * one[0] + am * one[1]
                if r1 is not None:
                    real = real + step * r1
                    imag = imag + step * i1
                if r2 is not None:
                    real = real - r2
                    imag = imag - i2
                state[n][4:] = [real, imag, r1, i1]
        for n in range(CHUNK):
            one, three, start, step, r0, i0, r1, i1 = state[n]
            real = r0 - r1 * three[0] - i1 * three[1]
            imag = i0 - i1 * three[0] + r1 * three[1]
            slope = real * start[0] - imag * start[1]
            for c in range(3):
                u = jnp.broadcast_to(dir_ref[0, :, c : c + 1], (8, 128))
                acc_ref[(at * CHUNK + n) * 3 + c] += u * slope
        return carry

    lax.fori_loop(0, LANE_GROUPS // CHUNK, chunk, 0, unroll=True)

    @pl.when(group == GROUPS - 1)
    def _():
        for j in range(LANE_GROUPS):
            lanes = slice(j % 2 * 128, j % 2 * 128 + 128)
            for c in range(3):
                out_ref[j // 2, c : c + 1, lanes] = jnp.sum(acc_ref[j * 3 + c], axis=0, keepdims=True) * (1.0 / TURN)


def kicks(position, points, directions, amplitude, intensity, shells):
    return pl.pallas_call(
        kick_kernel,
        grid_spec=pltpu.PrefetchScalarGridSpec(
            num_scalar_prefetch=1,
            grid=(GROUPS,),
            in_specs=[
                point_spec(),
                direction_spec(),
                pl.BlockSpec((1, 2, 8, 128), lambda g, p: (g, 0, 0, 0)),
                pl.BlockSpec((PARTS * REPLICAS, 128), lambda g, p: (0, 0)),
                pl.BlockSpec((2, 128), lambda g, p: (0, 0)),
            ],
            out_specs=pl.BlockSpec((PARTS, 3, SOL), lambda g, p: (0, 0, 0)),
            scratch_shapes=[
                pltpu.VMEM((6 * CENTERS, 8, 128), F32),
                pltpu.VMEM((8, 128), F32),
                pltpu.VMEM((LANE_GROUPS * 3, 8, 128), F32),
            ],
        ),
        out_shape=jax.ShapeDtypeStruct((PARTS, 3, SOL), F32),
        compiler_params=PARAMS,
        cost_estimate=pl.CostEstimate(flops=10_000_000_000, bytes_accessed=1_000_000, transcendentals=0),
        name="kicks",
    )(position, points, directions, amplitude, intensity, shells)


def exchange(head, tail):
    right = [(i, (i + 1) % PARTS) for i in range(PARTS)]
    left = [((i + 1) % PARTS, i) for i in range(PARTS)]
    return lax.ppermute(tail, "sp", right), lax.ppermute(head, "sp", left)


def to_all(value, axes):
    return lax.all_to_all(value, axes, 0, 0, tiled=True)


def shards(
    positions,
    velocities,
    strength,
    inv_mass,
    tile_lists,
    solute_index,
    scatter_weight,
    intensity_exp,
    precision,
):
    position = lax.axis_index("sp").astype(jnp.int32).reshape(1)
    directions = jnp.asarray(direction_table())
    tiles = tile_lists.reshape(-1)
    shells = jnp.stack([precision, intensity_exp]).reshape(2, CENTERS, 3)
    shells = jnp.pad(jnp.swapaxes(shells, 1, 2).reshape(2, NQ), ((0, 0), (0, 128 - NQ)))
    state, head, tail, first = pack(
        positions[0], strength, velocities[0], inv_mass, solute_index, scatter_weight
    )
    halo = exchange(head, tail)
    first = to_all(first, "sp")
    state, head, tail = pair_step(0, tiles, position, state, halo)
    halo = exchange(head, tail)
    amp, inten = amplitudes(position, first, directions)
    inten = to_all(inten, ("rep", "sp"))
    state, head, tail, second = pair_step(
        1, tiles, position, state, halo, solute_index, scatter_weight, gathers=True
    )
    halo = exchange(head, tail)
    second = to_all(second, "sp")
    kick = to_all(kicks(position, first, directions, amp, inten, shells), "sp")
    amp, inten = amplitudes(position, second, directions)
    inten = to_all(inten, ("rep", "sp"))
    state, head, tail = pair_step(2, tiles, position, state, halo, solute_index, scatter_weight, kick)
    halo = exchange(head, tail)
    kick = to_all(kicks(position, second, directions, amp, inten, shells), "sp")
    place, speed = pair_step(3, tiles, position, state, halo, last=True)
    speed = finish(speed, inv_mass, solute_index, scatter_weight, kick)
    return (place[None], speed[None])


def solution(mesh):
    in_specs = (
        P("rep", None, "sp"),
        P("rep", None, "sp"),
        P("rep", "sp"),
        P("rep", "sp"),
        P("rep", None, "sp", None),
        P("rep", "sp"),
        P("rep", "sp"),
        P(),
        P(),
    )
    out_specs = (P("rep", None, "sp"), P("rep", None, "sp"))
    return jax.shard_map(shards, mesh=mesh, in_specs=in_specs, out_specs=out_specs, check_vma=False)
```

time: 904 us -> 139 us (0.15)
  other arithmetic: 713 us -> 0.01 us
  Pallas kernels: 0 us -> 80.2 us
  waiting for transfers between devices: 56.1 us -> 0.18 us
  local copies, waits for them, and re-layouts: 49.9 us -> 5.01 us
  blocking collectives: 33.4 us -> 0 us
  starting transfers between devices: 25.1 us -> 52.1 us
  between operations: 15.1 us -> 0.85 us
    reduce_sum x59 -> x0, other arithmetic: 646 us -> none  [the longest x12 296 us: one_block(): jnp.sum(weights * jnp.cos(phases), axis=-1)]
    pallas_call x0 -> x10, Pallas kernels: none -> 80.2 us  [the longest x4 32.4 us: pair_step(): pl.pallas_call(functools.partial(pair_kernel, step, kicked, gathers, last...]
    all_to_all x0 -> x6, starting transfers between devices: none -> 43.9 us  [to_all(): return lax.all_to_all(value, axes, 0, 0, tiled=True)]
    psum x1 -> x0, waiting for transfers between devices: 43.6 us -> none  [shards(): amplitude = lax.psum(partial_value, 'sp')]
    psum x1 -> x0, blocking collectives: 33.4 us -> none  [shards(): intensity = lax.psum(shell_intensity(amplitude), 'rep') / replica_count]
    add x40 -> x0, other arithmetic: 33 us -> none  [the longest x3 21.4 us: shards(): coords_now = coords_now + TIME_STEP * speed_now]
    ppermute x8, starting transfers between devices: 25.1 us -> 8.24 us  [exchange(): return (lax.ppermute(tail, 'sp', right), lax.ppermute(head, 'sp', left))]
    ppermute x8, waiting for transfers between devices: 12.5 us -> 0.02 us  [exchange(): return (lax.ppermute(tail, 'sp', right), lax.ppermute(head, 'sp', left))]
  transfers between devices with their start and end apart: 9 -> 14, of which waited for: 4 -> 1; matrix products, arithmetic and copies ran while one was open for 4% -> 0% of each run, Pallas kernels for 0% -> 57%
where the time goes in v1:
time: 139 us; the launch traced here: 138 us
  Pallas kernels  80.2 us (58%)
  starting transfers between devices  52.1 us (37%)
  local copies, waits for them, and re-layouts  5.01 us (4%)
    all_to_all x6, starting transfers between devices, to_all(): return lax.all_to_all(value, axes, 0, 0, tiled=True)  43.9 us
    pallas_call x4, Pallas kernels, pair_step(): pl.pallas_call(functools.partial(pair_kernel, step, kicked, gathers, last...  32.4 us
    pallas_call x2, Pallas kernels, kicks(): pl.pallas_call(kick_kernel, grid_spec=pltpu.PrefetchScalarGridSpec(num_sc...  24.5 us
    pallas_call x2, Pallas kernels, amplitudes(): pl.pallas_call(amplitude_kernel, grid_spec=pltpu.PrefetchScalarGridSpec(n...  21.8 us
    ppermute x8, starting transfers between devices, exchange(): return (lax.ppermute(tail, 'sp', right), lax.ppermute(head, 'sp', left))  8.24 us
    unnamed x20, local copies, waits for them, and re-layouts  4.47 us
  transfers between devices with their start and end apart: 14, of which 1 were waited for; matrix products, arithmetic and copies ran while one was open for 0% of the time, Pallas kernels for 57%

profile of v1, /device:TPU:8, one launch (start us, length us, event | category | flops | bytes accessed | tf_op | source)
XLA Modules:
  0.0 138.4 jit_solution(10252093229096215546)
XLA Ops:
  0.6 0.0 copy-start
  0.6 0.0 copy-start.1
  0.7 0.0 copy-start.3
  0.7 1.1 copy_bitcast_fusion
  1.8 0.0 copy-start.2
  1.8 0.0 copy-done
  1.8 0.0 copy-done.1
  1.8 0.0 copy-done.3
  1.8 0.6 copy-done.2
  2.4 1.0 pack.1
  3.5 1.6 %collective-permute-start = (f32[4,4096]{1,0:T(4,128)S(1)}, f32[4,4096]{1,0:T(4,128)S(1)}, u32[]{:S(2)}, u32[]{:S(2)}) collective-permute-start(f32[4,4096]{1,0:T(4,128)S(1)} %get-tuple-element.23), channel_id=1, source_target_pairs={{0,1},{1,2},{2,3},{3,4},{4,5},{5,6},{6,7},{7,0},{8,9},{9,10},{10,1... | collective-permute-start | bytes 196616 | tf_op jit(solution)/shard_map/ppermute | solution.py:547
  5.1 0.4 collective-permute-start.1
  5.5 0.0 copy-start.5
  5.5 6.4 %all-to-all-start = ((f32[8,4,256]{2,1,0:T(4,128)}), f32[8,4,256]{2,1,0:T(4,128)S(1)}, u32[]{:S(2)}, u32[]{:S(2)}) async-start(f32[8,4,256]{2,1,0:T(4,128)} %get-tuple-element.31), calls=%async_computation | async-start | bytes 65536 | tf_op jit(solution)/shard_map/all_to_all | solution.py:551
  11.9 0.0 copy-done.5
  11.9 0.1 copy.19
  12.0 0.0 copy-start.6
  12.0 0.1 reshape.22.refs_0_
  12.2 0.5 copy-done.6
  12.7 0.1 stack.9
  12.8 0.0 copy-start.7
  12.8 0.1 copy.21
  12.9 0.6 copy-done.7
  13.4 0.1 stack.10
  13.5 0.1 copy.22
  13.6 0.1 reshape.24
  13.7 0.0 collective-permute-done.refs_3_
  13.7 0.0 collective-permute-done.1.refs_4_
  13.7 0.0 copy-start.4
  13.7 7.8 %pair_step.4 = (f32[8,8192]{1,0:T(8,128)S(1)}, f32[4,4096]{1,0:T(4,128)S(1)}, f32[4,4096]{1,0:T(4,128)S(1)}) custom-call(s32[1024]{0:T(1024)S(1)} %reshape.22.refs_0_, s32[1]{0:T(128)} %bitcast.refs_1_.position_ref, f32[8,8192]{1,0:T(8,128)S(1)} %get-tuple-element.22.refs_2_, f32[4,4096]{1,0:T(4,128)S(1)} %collective-permute-done.refs_3_, ...), custom_call_target="tpu_custom_call" | custom-call | flops 6000000000 | bytes 2000000 | tf_op jit(solution)/shard_map/pair_step/pallas_call | solution.py:325
  21.6 1.5 %collective-permute-start.2 = (f32[4,4096]{1,0:T(4,128)S(1)}, f32[4,4096]{1,0:T(4,128)S(1)}, u32[]{:S(2)}, u32[]{:S(2)}) collective-permute-start(f32[4,4096]{1,0:T(4,128)S(1)} %get-tuple-element.26), channel_id=1, source_target_pairs={{0,1},{1,2},{2,3},{3,4},{4,5},{5,6},{6,7},{7,0},{8,9},{9,10},{10,1... | collective-permute-start | bytes 196616 | tf_op jit(solution)/shard_map/ppermute | solution.py:547
  23.1 0.6 collective-permute-start.3
  23.7 0.0 all-to-all-done.point_ref
  23.7 0.0 copy-done.4
  23.7 10.9 %amplitudes.2 = (f32[13,2,8,128]{3,2,1,0:T(8,128)S(1)}, f32[128,128]{1,0:T(8,128)}) custom-call(s32[1]{0:T(128)} %bitcast.refs_1_.position_ref, f32[8,4,256]{2,1,0:T(4,128)S(1)} %all-to-all-done.point_ref, f32[8,104,3]{2,1,0:T(8,128)S(1)} %copy-done.4), custom_call_target="tpu_custom_call" | custom-call | flops 10000000000 | bytes 1000000 | tf_op jit(solution)/shard_map/amplitudes/pallas_call | solution.py:435
  34.6 9.9 %all-to-all-start.1 = ((f32[128,1,128]{2,1,0:T(1,128)}), f32[128,1,128]{2,1,0:T(1,128)S(1)}, u32[]{:S(2)}, u32[]{:S(2)}) async-start(f32[128,1,128]{2,1,0:T(1,128)} %bitcast.2), calls=%async_computation.1 | async-start | bytes 131072 | tf_op jit(solution)/shard_map/all_to_all | solution.py:551
  44.5 0.0 collective-permute-done.2.refs_3_
  44.5 0.0 collective-permute-done.3.refs_4_
  44.5 8.7 %pair_step.5 = (f32[8,8192]{1,0:T(8,128)S(1)}, f32[4,4096]{1,0:T(4,128)S(1)}, f32[4,4096]{1,0:T(4,128)S(1)}, f32[8,4,256]{2,1,0:T(4,128)}) custom-call(s32[1024]{0:T(1024)S(1)} %reshape.22.refs_0_, s32[1]{0:T(128)} %bitcast.refs_1_.position_ref, f32[8,8192]{1,0:T(8,128)S(1)} %get-tuple-element.25.refs_2_, f32[4,4096]{1,0:T(4,128)S(1)} %collective-permute-done.2.refs_3_, ...), custom_call_target="tpu_custom_call" | custom-call | flops 6000000000 | bytes 2000000 | tf_op jit(solution)/shard_map/pair_step/pallas_call | solution.py:325
  53.2 0.1 all-to-all-done.1
  53.3 5.8 %all-to-all-start.3 = ((f32[8,4,256]{2,1,0:T(4,128)}), f32[8,4,256]{2,1,0:T(4,128)S(1)}, u32[]{:S(2)}, u32[]{:S(2)}) async-start(f32[8,4,256]{2,1,0:T(4,128)} %get-tuple-element.39), calls=%async_computation.3 | async-start | bytes 65536 | tf_op jit(solution)/shard_map/all_to_all | solution.py:551
  59.1 12.2 %kicks.2 = f32[8,3,256]{2,1,0:T(4,128)} custom-call(s32[1]{0:T(128)} %bitcast.refs_1_.position_ref, f32[8,4,256]{2,1,0:T(4,128)S(1)} %all-to-all-done.point_ref, f32[8,104,3]{2,1,0:T(8,128)S(1)} %copy-done.4, f32[13,2,8,128]{3,2,1,0:T(8,128)S(1)} %get-tuple-element.32.amp_ref, f32[128,128]{1,0:T(8,128)S(1)} %bitcast.22, f32[2,128]{1,0:T(2,128)S(1)} %pad.4.shell_ref), custom_call_target="tpu_custom_call" | custom-call | flops 10000000000 | bytes 1000000 | tf_op jit(solution)/shard_map/kicks/pallas_call | solution.py:518
  71.4 1.5 %collective-permute-start.4 = (f32[4,4096]{1,0:T(4,128)S(1)}, f32[4,4096]{1,0:T(4,128)S(1)}, u32[]{:S(2)}, u32[]{:S(2)}) collective-permute-start(f32[4,4096]{1,0:T(4,128)S(1)} %get-tuple-element.29), channel_id=1, source_target_pairs={{0,1},{1,2},{2,3},{3,4},{4,5},{5,6},{6,7},{7,0},{8,9},{9,10},{10,1... | collective-permute-start | bytes 196616 | tf_op jit(solution)/shard_map/ppermute | solution.py:547
  72.8 0.6 collective-permute-start.5
  73.4 0.0 all-to-all-done.3.point_ref
  73.4 5.7 %all-to-all-start.2 = ((f32[8,3,256]{2,1,0:T(4,128)}), f32[8,3,256]{2,1,0:T(4,128)S(1)}, u32[]{:S(2)}, u32[]{:S(2)}) async-start(f32[8,3,256]{2,1,0:T(4,128)} %kicks.2), calls=%async_computation.2 | async-start | bytes 65536 | tf_op jit(solution)/shard_map/all_to_all | solution.py:551
  79.1 10.9 %amplitudes.3 = (f32[13,2,8,128]{3,2,1,0:T(8,128)S(1)}, f32[128,128]{1,0:T(8,128)}) custom-call(s32[1]{0:T(128)} %bitcast.refs_1_.position_ref, f32[8,4,256]{2,1,0:T(4,128)S(1)} %all-to-all-done.3.point_ref, f32[8,104,3]{2,1,0:T(8,128)S(1)} %copy-done.4), custom_call_target="tpu_custom_call" | custom-call | flops 10000000000 | bytes 1000000 | tf_op jit(solution)/shard_map/amplitudes/pallas_call | solution.py:435
  90.0 0.0 all-to-all-done.2.refs_7_
  90.0 9.5 %all-to-all-start.4 = ((f32[128,1,128]{2,1,0:T(1,128)}), f32[128,1,128]{2,1,0:T(1,128)S(1)}, u32[]{:S(2)}, u32[]{:S(2)}) async-start(f32[128,1,128]{2,1,0:T(1,128)} %bitcast.7), calls=%async_computation.4 | async-start | bytes 131072 | tf_op jit(solution)/shard_map/all_to_all | solution.py:551
  99.5 0.0 collective-permute-done.4.refs_3_
  99.5 0.0 collective-permute-done.5.refs_4_
  99.5 8.2 %pair_step.6 = (f32[8,8192]{1,0:T(8,128)S(1)}, f32[4,4096]{1,0:T(4,128)S(1)}, f32[4,4096]{1,0:T(4,128)S(1)}) custom-call(s32[1024]{0:T(1024)S(1)} %reshape.22.refs_0_, s32[1]{0:T(128)} %bitcast.refs_1_.position_ref, f32[8,8192]{1,0:T(8,128)S(1)} %get-tuple-element.28.refs_2_, f32[4,4096]{1,0:T(4,128)S(1)} %collective-permute-done.4.refs_3_, ...), custom_call_target="tpu_custom_call" | custom-call | flops 6000000000 | bytes 2000000 | tf_op jit(solution)/shard_map/pair_step/pallas_call | solution.py:325
  107.7 1.5 %collective-permute-start.6 = (f32[4,4096]{1,0:T(4,128)S(1)}, f32[4,4096]{1,0:T(4,128)S(1)}, u32[]{:S(2)}, u32[]{:S(2)}) collective-permute-start(f32[4,4096]{1,0:T(4,128)S(1)} %get-tuple-element.35), channel_id=1, source_target_pairs={{0,1},{1,2},{2,3},{3,4},{4,5},{5,6},{6,7},{7,0},{8,9},{9,10},{10,1... | collective-permute-start | bytes 196616 | tf_op jit(solution)/shard_map/ppermute | solution.py:547
  109.2 0.6 collective-permute-start.7
  109.8 0.0 all-to-all-done.4
  109.8 12.2 %kicks.3 = f32[8,3,256]{2,1,0:T(4,128)} custom-call(s32[1]{0:T(128)} %bitcast.refs_1_.position_ref, f32[8,4,256]{2,1,0:T(4,128)S(1)} %all-to-all-done.3.point_ref, f32[8,104,3]{2,1,0:T(8,128)S(1)} %copy-done.4, f32[13,2,8,128]{3,2,1,0:T(8,128)S(1)} %get-tuple-element.40.amp_ref, f32[128,128]{1,0:T(8,128)S(1)} %bitcast.21, f32[2,128]{1,0:T(2,128)S(1)} %pad.4.shell_ref), custom_call_target="tpu_custom_call" | custom-call | flops 10000000000 | bytes 1000000 | tf_op jit(solution)/shard_map/kicks/pallas_call | solution.py:518
  122.0 6.6 %all-to-all-start.5 = ((f32[8,3,256]{2,1,0:T(4,128)}), f32[8,3,256]{2,1,0:T(4,128)S(1)}, u32[]{:S(2)}, u32[]{:S(2)}) async-start(f32[8,3,256]{2,1,0:T(4,128)} %kicks.3), calls=%async_computation.5 | async-start | bytes 65536 | tf_op jit(solution)/shard_map/all_to_all | solution.py:551
  128.6 0.0 collective-permute-done.6.refs_3_
  128.6 0.0 collective-permute-done.7.refs_4_
  128.6 7.8 %pair_step.7 = (f32[3,8192]{1,0:T(4,128)S(1)}, f32[3,8192]{1,0:T(4,128)S(1)}) custom-call(s32[1024]{0:T(1024)S(1)} %reshape.22.refs_0_, s32[1]{0:T(128)} %bitcast.refs_1_.position_ref, f32[8,8192]{1,0:T(8,128)S(1)} %get-tuple-element.34.refs_2_, f32[4,4096]{1,0:T(4,128)S(1)} %collective-permute-done.6.refs_3_, f32[4,4096]{1,0:T(4,128)S(1)} %collective-permute-done.7.refs_4_), custom_call_target="tpu_custom_call" | custom-call | flops 6000000000 | bytes 2000000 | tf_op jit(solution)/shard_map/pair_step/pallas_call | solution.py:325
  136.4 0.0 all-to-all-done.5.kick_ref
  136.4 0.5 finish.1
  136.9 0.7 copy.26
  137.7 0.7 copy.25
  (3 shorter events, 0.0 us)
Async XLA Ops:
  0.6 1.1 copy-start
  0.6 1.1 copy-start.1
  0.7 1.1 copy-start.3
  1.8 0.7 copy-start.2
  3.5 10.2 %collective-permute-start = (f32[4,4096]{1,0:T(4,128)S(1)}, f32[4,4096]{1,0:T(4,128)S(1)}, u32[]{:S(2)}, u32[]{:S(2)}) collective-permute-start(f32[4,4096]{1,0:T(4,128)S(1)} %get-tuple-element.23), channel_id=1, source_target_pairs={{0,1},{1,2},{2,3},{3,4},{4,5},{5,6},{6,7},{7,0},{8,9},{9,10},{10,1... | collective-permute-start | bytes 196616 | tf_op jit(solution)/shard_map/ppermute | solution.py:547
  5.1 8.7 %collective-permute-start.1 = (f32[4,4096]{1,0:T(4,128)S(1)}, f32[4,4096]{1,0:T(4,128)S(1)}, u32[]{:S(2)}, u32[]{:S(2)}) collective-permute-start(f32[4,4096]{1,0:T(4,128)S(1)} %get-tuple-element.24), channel_id=1, source_target_pairs={{1,0},{2,1},{3,2},{4,3},{5,4},{6,5},{7,6},{0,7},{9,8},{10,9},{11,1... | collective-permute-start | bytes 196616 | tf_op jit(solution)/shard_map/ppermute | solution.py:547
  5.5 6.4 %copy-start.5 = (s32[1,4,64,4]{2,3,1,0:T(4,128)S(1)}, s32[1,4,64,4]{2,3,1,0:T(4,128)}, u32[]{:S(2)}) copy-start(s32[1,4,64,4]{2,3,1,0:T(4,128)} %param.14) | copy-start | bytes 12292
  5.5 18.2 %all-to-all-start = ((f32[8,4,256]{2,1,0:T(4,128)}), f32[8,4,256]{2,1,0:T(4,128)S(1)}, u32[]{:S(2)}, u32[]{:S(2)}) async-start(f32[8,4,256]{2,1,0:T(4,128)} %get-tuple-element.31), calls=%async_computation | async-start | bytes 65536 | tf_op jit(solution)/shard_map/all_to_all | solution.py:551
  12.0 0.7 copy-start.6
  12.8 0.7 copy-start.7
  13.7 9.9 %copy-start.4 = (f32[8,104,3]{2,1,0:T(8,128)S(1)}, f32[8,104,3]{2,1,0:T(8,128)}, u32[]{:S(2)}) copy-start(f32[8,104,3]{2,1,0:T(8,128)} %constant.9.clone.dir_ref) | copy-start | bytes 29956
  21.6 22.9 %collective-permute-start.2 = (f32[4,4096]{1,0:T(4,128)S(1)}, f32[4,4096]{1,0:T(4,128)S(1)}, u32[]{:S(2)}, u32[]{:S(2)}) collective-permute-start(f32[4,4096]{1,0:T(4,128)S(1)} %get-tuple-element.26), channel_id=1, source_target_pairs={{0,1},{1,2},{2,3},{3,4},{4,5},{5,6},{6,7},{7,0},{8,9},{9,10},{10,1... | collective-permute-start | bytes 196616 | tf_op jit(solution)/shard_map/ppermute | solution.py:547
  23.1 21.4 %collective-permute-start.3 = (f32[4,4096]{1,0:T(4,128)S(1)}, f32[4,4096]{1,0:T(4,128)S(1)}, u32[]{:S(2)}, u32[]{:S(2)}) collective-permute-start(f32[4,4096]{1,0:T(4,128)S(1)} %get-tuple-element.27), channel_id=1, source_target_pairs={{1,0},{2,1},{3,2},{4,3},{5,4},{6,5},{7,6},{0,7},{9,8},{10,9},{11,1... | collective-permute-start | bytes 196616 | tf_op jit(solution)/shard_map/ppermute | solution.py:547
  34.6 18.7 %all-to-all-start.1 = ((f32[128,1,128]{2,1,0:T(1,128)}), f32[128,1,128]{2,1,0:T(1,128)S(1)}, u32[]{:S(2)}, u32[]{:S(2)}) async-start(f32[128,1,128]{2,1,0:T(1,128)} %bitcast.2), calls=%async_computation.1 | async-start | bytes 131072 | tf_op jit(solution)/shard_map/all_to_all | solution.py:551
  53.3 20.1 %all-to-all-start.3 = ((f32[8,4,256]{2,1,0:T(4,128)}), f32[8,4,256]{2,1,0:T(4,128)S(1)}, u32[]{:S(2)}, u32[]{:S(2)}) async-start(f32[8,4,256]{2,1,0:T(4,128)} %get-tuple-element.39), calls=%async_computation.3 | async-start | bytes 65536 | tf_op jit(solution)/shard_map/all_to_all | solution.py:551
  71.4 28.2 %collective-permute-start.4 = (f32[4,4096]{1,0:T(4,128)S(1)}, f32[4,4096]{1,0:T(4,128)S(1)}, u32[]{:S(2)}, u32[]{:S(2)}) collective-permute-start(f32[4,4096]{1,0:T(4,128)S(1)} %get-tuple-element.29), channel_id=1, source_target_pairs={{0,1},{1,2},{2,3},{3,4},{4,5},{5,6},{6,7},{7,0},{8,9},{9,10},{10,1... | collective-permute-start | bytes 196616 | tf_op jit(solution)/shard_map/ppermute | solution.py:547
  72.8 26.7 %collective-permute-start.5 = (f32[4,4096]{1,0:T(4,128)S(1)}, f32[4,4096]{1,0:T(4,128)S(1)}, u32[]{:S(2)}, u32[]{:S(2)}) collective-permute-start(f32[4,4096]{1,0:T(4,128)S(1)} %get-tuple-element.30), channel_id=1, source_target_pairs={{1,0},{2,1},{3,2},{4,3},{5,4},{6,5},{7,6},{0,7},{9,8},{10,9},{11,1... | collective-permute-start | bytes 196616 | tf_op jit(solution)/shard_map/ppermute | solution.py:547
  73.4 16.6 %all-to-all-start.2 = ((f32[8,3,256]{2,1,0:T(4,128)}), f32[8,3,256]{2,1,0:T(4,128)S(1)}, u32[]{:S(2)}, u32[]{:S(2)}) async-start(f32[8,3,256]{2,1,0:T(4,128)} %kicks.2), calls=%async_computation.2 | async-start | bytes 65536 | tf_op jit(solution)/shard_map/all_to_all | solution.py:551
  90.0 19.8 %all-to-all-start.4 = ((f32[128,1,128]{2,1,0:T(1,128)}), f32[128,1,128]{2,1,0:T(1,128)S(1)}, u32[]{:S(2)}, u32[]{:S(2)}) async-start(f32[128,1,128]{2,1,0:T(1,128)} %bitcast.7), calls=%async_computation.4 | async-start | bytes 131072 | tf_op jit(solution)/shard_map/all_to_all | solution.py:551
  107.7 20.9 %collective-permute-start.6 = (f32[4,4096]{1,0:T(4,128)S(1)}, f32[4,4096]{1,0:T(4,128)S(1)}, u32[]{:S(2)}, u32[]{:S(2)}) collective-permute-start(f32[4,4096]{1,0:T(4,128)S(1)} %get-tuple-element.35), channel_id=1, source_target_pairs={{0,1},{1,2},{2,3},{3,4},{4,5},{5,6},{6,7},{7,0},{8,9},{9,10},{10,1... | collective-permute-start | bytes 196616 | tf_op jit(solution)/shard_map/ppermute | solution.py:547
  109.2 19.4 %collective-permute-start.7 = (f32[4,4096]{1,0:T(4,128)S(1)}, f32[4,4096]{1,0:T(4,128)S(1)}, u32[]{:S(2)}, u32[]{:S(2)}) collective-permute-start(f32[4,4096]{1,0:T(4,128)S(1)} %get-tuple-element.36), channel_id=1, source_target_pairs={{1,0},{2,1},{3,2},{4,3},{5,4},{6,5},{7,6},{0,7},{9,8},{10,9},{11,1... | collective-permute-start | bytes 196616 | tf_op jit(solution)/shard_map/ppermute | solution.py:547
  122.0 14.4 %all-to-all-start.5 = ((f32[8,3,256]{2,1,0:T(4,128)}), f32[8,3,256]{2,1,0:T(4,128)S(1)}, u32[]{:S(2)}, u32[]{:S(2)}) async-start(f32[8,3,256]{2,1,0:T(4,128)} %kicks.3), calls=%async_computation.5 | async-start | bytes 65536 | tf_op jit(solution)/shard_map/all_to_all | solution.py:551

commit v2 on v1

--- a/solution.py
+++ b/solution.py
@@ -29,7 +29,8 @@
 REPLICAS = 16
 DIR_PART = M // PARTS
 GROUPS = -(-DIR_PART // 8)
-CENTERS = NQ // 3
+SIDE = 4
+CENTERS = NQ // (2 * SIDE)
 LANE_GROUPS = PARTS * SOL // 128
 CHUNK = 4
 FILL_UNROLL = 16
@@ -38,7 +39,7 @@
 ALPHA = math.sqrt(HALF_INVERSE * math.log2(math.e))
 COUPLING = PAIR_STRENGTH / math.sqrt(NEIGHBOURS * BLOCK)
 NORM = 1.0 / math.sqrt(PARTS * SOL)
-TURN = 1.0 / (32.0 * math.pi)
+TURN = 1.0 / (64.0 * math.pi)
 
 F32 = jnp.float32
 BF16 = jnp.bfloat16
@@ -50,8 +51,11 @@
     radius = np.sqrt(1.0 - height * height)
     azimuth = (order * 610 % 987) * (2.0 * math.pi / 987.0)
     rows = np.stack([radius * np.cos(azimuth), radius * np.sin(azimuth), height], axis=-1) * TURN
-    table = np.zeros((PARTS, GROUPS * 8, 3), np.float32)
-    table[:, :DIR_PART] = rows.reshape(PARTS, DIR_PART, 3)
+    padded = np.zeros((PARTS, GROUPS * 8, 3), np.float32)
+    padded[:, :DIR_PART] = rows.reshape(PARTS, DIR_PART, 3)
+    table = np.zeros((PARTS, 8, 128), np.float32)
+    for c in range(3):
+        table[:, :, 16 * c : 16 * c + GROUPS] = np.swapaxes(padded[:, :, c].reshape(PARTS, GROUPS, 8), 1, 2)
     return table
 
 
@@ -355,72 +359,112 @@
     one = double(*double(cos, sin))
     two = double(*one)
     three = product(two, one)
+    five = product(three, two)
+    seven = product(five, two)
     sixteen = double(*double(*double(*two)))
-    return one, three, product(sixteen, one)
-
-
-def group_turns(dir_ref, point_ref, part, half):
+    return [one, three, five, seven], sixteen, product(double(*sixteen), seven)
+
+
+def halves(value):
+    high = value.astype(BF16)
+    return high, (value - high.astype(F32)).astype(BF16)
+
+
+def term_rows(powers):
+    values = [p[0] for p in powers] + [p[1] for p in powers]
+    parts = [halves(jnp.concatenate(values[i : i + 2], axis=0)) for i in range(0, 8, 2)]
+    return [p[0] for p in parts], [p[1] for p in parts]
+
+
+def group_directions(dir_ref, group):
+    lane = lax.broadcasted_iota(jnp.int32, (8, 128), 1)
+
+    def one(c):
+        column = jnp.sum(jnp.where(lane == 16 * c + group, dir_ref[0], 0.0), axis=1, keepdims=True)
+        return jnp.broadcast_to(column, (8, 128))
+
+    return [one(c) for c in range(3)]
+
+
+def group_turns(u, point_ref, part, half):
     lanes = slice(half * 128, half * 128 + 128)
 
     def coordinate(c):
         return jnp.broadcast_to(point_ref[part, c : c + 1, lanes], (8, 128))
 
-    u = [jnp.broadcast_to(dir_ref[0, :, c : c + 1], (8, 128)) for c in range(3)]
     return u[0] * coordinate(0) + u[1] * coordinate(1) + u[2] * coordinate(2), coordinate(3)
 
 
-def amplitude_kernel(position_ref, point_ref, dir_ref, amp_ref, inten_ref, acc_ref, square_ref):
+def amplitude_kernel(position_ref, point_ref, dir_ref, amp_ref, inten_ref, total_ref):
     group = pl.program_id(0)
-    zero = jnp.zeros((8, 128), F32)
-
-    @pl.when(group == 0)
-    def _():
-        square_ref[...] = zero
-
-    for i in range(6 * CENTERS):
-        acc_ref[i] = zero
-
-    def chunk(at, carry):
-        state = []
+    row = rows_of((8, 128))
+    lane = lax.broadcasted_iota(jnp.int32, (8, 128), 1)
+
+    u = group_directions(dir_ref, group)
+    total = None
+    for at in range(LANE_GROUPS // CHUNK):
+        left = []
+        right = []
         for n in range(CHUNK):
-            turns, weight = group_turns(dir_ref, point_ref, at * (CHUNK // 2) + n // 2, n % 2)
-            one, three, start = unit_powers(turns)
-            now = (weight * start[0], weight * start[1])
-            before = product_conj(now, three)
-            state.append([one[0], one[1], three[0] + three[0], now[0], now[1], before[0], before[1]])
-        for k in range(CENTERS):
-            sums = None
-            for n in range(CHUNK):
-                c1, s1, step, c, s, cb, sb = state[n]
-                terms = [c, s, c * c1, s * s1, s * c1, c * s1]
-                sums = terms if sums is None else [p + q for p, q in zip(sums, terms)]
+            j = at * CHUNK + n
+            turns, weight = group_turns(u, point_ref, j // 2, j % 2)
+            powers, step, start = unit_powers(turns)
+            high, low = term_rows(powers)
+            right.append(jnp.concatenate(high + low, axis=0))
+            c, s = weight * start[0], weight * start[1]
+            cb, sb = product_conj((c, s), step)
+            twice = step[0] + step[0]
+            tops = []
+            bottoms = []
+            for k in range(CENTERS):
+                top, bottom = halves(jnp.concatenate([c, s], axis=0))
+                tops.append(top)
+                bottoms.append(bottom)
                 if k + 1 < CENTERS:
-                    state[n][3:] = [step * c - cb, step * s - sb, c, s]
-            for i in range(6):
-                acc_ref[6 * k + i] += sums[i]
-        return carry
-
-    lax.fori_loop(0, LANE_GROUPS // CHUNK, chunk, 0, unroll=True)
-
-    lane = lax.broadcasted_iota(jnp.int32, (8, 128), 1)
-    inside = rows_of((8, 128)) + group * 8 < DIR_PART
-    real = zero
-    imag = zero
-    for k in range(CENTERS):
-        c, s, t1, t2, t3, t4 = [acc_ref[6 * k + i] for i in range(6)]
-        for i, (a, b) in enumerate([(t1 + t2, t3 - t4), (c, s), (t1 - t2, t3 + t4)]):
-            here = lane == 16 * i + k
-            real = jnp.where(here, jnp.sum(a, axis=1, keepdims=True), real)
-            imag = jnp.where(here, jnp.sum(b, axis=1, keepdims=True), imag)
-    real = real * NORM
-    imag = imag * NORM
-    amp_ref[0, 0] = real
-    amp_ref[0, 1] = imag
-    square_ref[...] += jnp.where(inside, real * real + imag * imag, 0.0)
+                    c, s, cb, sb = twice * c - cb, twice * s - sb, c, s
+            left.append(jnp.concatenate(tops + bottoms, axis=0))
+        part = lax.dot_general(
+            jnp.concatenate(left, axis=1),
+            jnp.concatenate(right, axis=1),
+            (((1,), (1,)), ((), ())),
+            preferred_element_type=F32,
+        )
+        total = part if total is None else total + part
+    total_ref[group] = total[0 : 16 * CENTERS] + total[16 * CENTERS :]
 
     @pl.when(group == GROUPS - 1)
     def _():
-        inten_ref[...] = jnp.broadcast_to(jnp.sum(square_ref[...], axis=0, keepdims=True), inten_ref.shape)
+        own = (lane & 7) == row
+        front = lane < 8 * SIDE
+        squares = [jnp.zeros((8, 128), F32)] * 2
+        for g in range(GROUPS):
+            real = jnp.zeros((8, 128), F32)
+            imag = real
+            for k in range(CENTERS):
+                c = jnp.sum(jnp.where(own, total_ref[g, 16 * k : 16 * k + 8], 0.0), axis=0, keepdims=True)
+                s = jnp.sum(jnp.where(own, total_ref[g, 16 * k + 8 : 16 * k + 16], 0.0), axis=0, keepdims=True)
+                real = jnp.where(row == k, c, real)
+                imag = jnp.where(row == k, s, imag)
+            real = (real + pltpu.roll(real, 64, axis=1)) * NORM
+            imag = (imag + pltpu.roll(imag, 64, axis=1)) * NORM
+            real_sin = pltpu.roll(real, 96, axis=1)
+            imag_sin = pltpu.roll(imag, 96, axis=1)
+            planes = [real - imag_sin, real + imag_sin, imag + real_sin, imag - real_sin]
+            inside = front & ((lane & 7) + g * 8 < DIR_PART)
+            planes = [jnp.where(inside, p, 0.0) for p in planes]
+            for i in range(4):
+                amp_ref[g, i] = planes[i]
+            for i in range(2):
+                squares[i] = squares[i] + planes[i] * planes[i] + planes[i + 2] * planes[i + 2]
+        spread = jnp.zeros((8, 128), F32)
+        for i in range(2):
+            square = squares[i]
+            for shift in (1, 2, 4):
+                square = square + pltpu.roll(square, 128 - shift, axis=1)
+            square = jnp.where(front & ((lane & 7) == 0), square, 0.0)
+            for k in range(CENTERS):
+                spread = spread + pltpu.roll(jnp.where(row == k, square, 0.0), 32 * i + k, axis=1)
+        inten_ref[...] = jnp.broadcast_to(jnp.sum(spread, axis=0, keepdims=True), inten_ref.shape)
 
 
 def point_spec():
@@ -428,7 +472,7 @@
 
 
 def direction_spec():
-    return pl.BlockSpec((1, 8, 3), lambda g, p: (p[0], g, 0))
+    return pl.BlockSpec((1, 8, 128), lambda g, p: (p[0], 0, 0))
 
 
 def amplitudes(position, points, directions):
@@ -439,13 +483,13 @@
             grid=(GROUPS,),
             in_specs=[point_spec(), direction_spec()],
             out_specs=[
-                pl.BlockSpec((1, 2, 8, 128), lambda g, p: (g, 0, 0, 0)),
+                pl.BlockSpec((GROUPS, 4, 8, 128), lambda g, p: (0, 0, 0, 0)),
                 pl.BlockSpec((PARTS * REPLICAS, 128), lambda g, p: (0, 0)),
             ],
-            scratch_shapes=[pltpu.VMEM((6 * CENTERS, 8, 128), F32), pltpu.VMEM((8, 128), F32)],
+            scratch_shapes=[pltpu.VMEM((GROUPS, 16 * CENTERS, 128), F32)],
         ),
         out_shape=[
-            jax.ShapeDtypeStruct((GROUPS, 2, 8, 128), F32),
+            jax.ShapeDtypeStruct((GROUPS, 4, 8, 128), F32),
             jax.ShapeDtypeStruct((PARTS * REPLICAS, 128), F32),
         ],
         compiler_params=PARAMS,
@@ -454,57 +498,83 @@
     )(position, points, directions)
 
 
-def kick_kernel(position_ref, point_ref, dir_ref, amp_ref, inten_ref, shell_ref, out_ref, coef_ref, scale_ref, acc_ref):
+def kick_kernel(position_ref, point_ref, dir_ref, amp_ref, inten_ref, shell_ref, out_ref, coef_ref, acc_ref):
     group = pl.program_id(0)
+    row = rows_of((8, 128))
+    lane = lax.broadcasted_iota(jnp.int32, (8, 128), 1)
 
     @pl.when(group == 0)
     def _():
         intensity = jnp.sum(inten_ref[...], axis=0, keepdims=True) * (1.0 / (M * REPLICAS))
-        lane = lax.broadcasted_iota(jnp.int32, (1, 128), 1)
-        shell = 1.0 + (3 * (lane & 15) + lax.shift_right_logical(lane, 4)).astype(F32) * (3.0 / NQ)
-        factor = shell_ref[0:1] * (intensity - shell_ref[1:2]) * (2.0 / M) * shell
-        scale_ref[...] = jnp.broadcast_to(factor, (8, 128))
-        for i in range(LANE_GROUPS * 3):
-            acc_ref[i] = jnp.zeros((8, 128), F32)
-
-    b = amp_ref[0, 0] * scale_ref[...]
-    a = amp_ref[0, 1] * scale_ref[...]
-    for k in range(CENTERS):
-        ax = [jnp.broadcast_to(a[:, 16 * i + k : 16 * i + k + 1], (8, 128)) for i in range(3)]
-        bx = [jnp.broadcast_to(b[:, 16 * i + k : 16 * i + k + 1], (8, 128)) for i in range(3)]
-        for i, v in enumerate([ax[1], ax[0] + ax[2], bx[0] - bx[2], bx[1], bx[0] + bx[2], ax[2] - ax[0]]):
-            coef_ref[6 * k + i] = v
-
-    def chunk(at, carry):
+        at = lax.broadcasted_iota(jnp.int32, (1, 128), 1)
+        offset = lax.shift_right_logical(at, 3) & 3
+        shell = 8 * (at & 7) + jnp.where((at & 32) == 0, 4 + offset, 3 - offset)
+        q = 1.0 + shell.astype(F32) * (3.0 / NQ)
+        factor = shell_ref[0:1] * (intensity - shell_ref[1:2]) * (2.0 / M) * q
+        scales = []
+        for i in range(2):
+            scale = jnp.zeros((8, 128), F32)
+            for k in range(CENTERS):
+                for o in range(SIDE):
+                    source = 32 * i + 8 * o + k
+                    here = (row == k) & (lax.shift_right_logical(lane, 3) == o)
+                    scale = jnp.where(here, jnp.broadcast_to(factor[:, source : source + 1], (8, 128)), scale)
+            scales.append(scale)
+        acc_ref[...] = jnp.zeros(acc_ref.shape, F32)
+        front = lane < 8 * SIDE
+        own = (lane & 7) == row
+        for g in range(GROUPS):
+            b_up = amp_ref[g, 0] * scales[0]
+            b_down = amp_ref[g, 1] * scales[1]
+            a_up = amp_ref[g, 2] * scales[0]
+            a_down = amp_ref[g, 3] * scales[1]
+            real = jnp.where(front, a_up + a_down, pltpu.roll(b_down - b_up, 32, axis=1))
+            imag = jnp.where(front, b_up + b_down, pltpu.roll(a_up - a_down, 32, axis=1))
+            tops = []
+            bottoms = []
+            for v in (real, imag):
+                high = v.astype(BF16).astype(F32)
+                tops.append(high + pltpu.roll(high, 64, axis=1))
+                bottoms.append(v - high)
+            for k in range(CENTERS):
+                at = slice(16 * k, 16 * k + 16)
+                first = jnp.concatenate([jnp.where(own, v[k : k + 1], 0.0) for v in tops], axis=0).astype(BF16)
+                last = jnp.concatenate([jnp.where(own, v[k : k + 1], 0.0) for v in bottoms], axis=0).astype(BF16)
+                coef_ref[g, at, 0:128] = first
+                coef_ref[g, at, 128:256] = last
+
+    u = group_directions(dir_ref, group)
+
+    for at in range(LANE_GROUPS // CHUNK):
         state = []
+        columns = []
         for n in range(CHUNK):
-            turns, _ = group_turns(dir_ref, point_ref, at * (CHUNK // 2) + n // 2, n % 2)
-            one, three, start = unit_powers(turns)
-            state.append([one, three, start, three[0] + three[0], None, None, None, None])
-        for k in range(CENTERS - 1, -1, -1):
-            a1, ap, bm, b1, bp, am = [coef_ref[6 * k + i] for i in range(6)]
-            for n in range(CHUNK):
-                one, three, start, step, r1, i1, r2, i2 = state[n]
-                real = a1 + ap * one[0] + bm * one[1]
-                imag = b1 + bp * one[0] + am * one[1]
+            j = at * CHUNK + n
+            turns, _ = group_turns(u, point_ref, j // 2, j % 2)
+            powers, step, start = unit_powers(turns)
+            high, low = term_rows(powers)
+            columns.append(jnp.concatenate(high + low + high, axis=0))
+            state.append([step, start, step[0] + step[0]])
+        terms = jnp.dot(coef_ref[group, :, 0:192], jnp.concatenate(columns, axis=1), preferred_element_type=F32)
+        for n in range(CHUNK):
+            step, start, twice = state[n]
+            lanes = slice(n * 128, n * 128 + 128)
+            r1 = i1 = r2 = i2 = None
+            for k in range(CENTERS - 1, -1, -1):
+                real = terms[16 * k : 16 * k + 8, lanes]
+                imag = terms[16 * k + 8 : 16 * k + 16, lanes]
                 if r1 is not None:
-                    real = real + step * r1
-                    imag = imag + step * i1
+                    real = real + twice * r1
+                    imag = imag + twice * i1
                 if r2 is not None:
                     real = real - r2
                     imag = imag - i2
-                state[n][4:] = [real, imag, r1, i1]
-        for n in range(CHUNK):
-            one, three, start, step, r0, i0, r1, i1 = state[n]
-            real = r0 - r1 * three[0] - i1 * three[1]
-            imag = i0 - i1 * three[0] + r1 * three[1]
+                r1, i1, r2, i2 = real, imag, r1, i1
+            real = r1 - r2 * step[0] - i2 * step[1]
+            imag = i1 - i2 * step[0] + r2 * step[1]
             slope = real * start[0] - imag * start[1]
             for c in range(3):
-                u = jnp.broadcast_to(dir_ref[0, :, c : c + 1], (8, 128))
-                acc_ref[(at * CHUNK + n) * 3 + c] += u * slope
-        return carry
-
-    lax.fori_loop(0, LANE_GROUPS // CHUNK, chunk, 0, unroll=True)
+                acc_ref[(at * CHUNK + n) * 3 + c] += u[c] * slope
 
     @pl.when(group == GROUPS - 1)
     def _():
@@ -523,14 +593,13 @@
             in_specs=[
                 point_spec(),
                 direction_spec(),
-                pl.BlockSpec((1, 2, 8, 128), lambda g, p: (g, 0, 0, 0)),
+                pl.BlockSpec((GROUPS, 4, 8, 128), lambda g, p: (0, 0, 0, 0)),
                 pl.BlockSpec((PARTS * REPLICAS, 128), lambda g, p: (0, 0)),
                 pl.BlockSpec((2, 128), lambda g, p: (0, 0)),
             ],
             out_specs=pl.BlockSpec((PARTS, 3, SOL), lambda g, p: (0, 0, 0)),
             scratch_shapes=[
-                pltpu.VMEM((6 * CENTERS, 8, 128), F32),
-                pltpu.VMEM((8, 128), F32),
+                pltpu.VMEM((GROUPS, 16 * CENTERS, 256), BF16),
                 pltpu.VMEM((LANE_GROUPS * 3, 8, 128), F32),
             ],
         ),
@@ -565,8 +634,9 @@
     position = lax.axis_index("sp").astype(jnp.int32).reshape(1)
     directions = jnp.asarray(direction_table())
     tiles = tile_lists.reshape(-1)
-    shells = jnp.stack([precision, intensity_exp]).reshape(2, CENTERS, 3)
-    shells = jnp.pad(jnp.swapaxes(shells, 1, 2).reshape(2, NQ), ((0, 0), (0, 128 - NQ)))
+    shells = jnp.stack([precision, intensity_exp]).reshape(2, CENTERS, 2, SIDE)
+    shells = jnp.stack([shells[:, :, 1], shells[:, :, 0, ::-1]], axis=1)
+    shells = jnp.pad(jnp.swapaxes(shells, 2, 3), ((0, 0), (0, 2), (0, 0), (0, 8 - CENTERS))).reshape(2, 128)
     state, head, tail, first = pack(
         positions[0], strength, velocities[0], inv_mass, solute_index, scatter_weight
     )

time: 139 us -> 126 us (0.906)
  Pallas kernels: 80.2 us -> 66.7 us
    pallas_call x2, Pallas kernels: 24.5 us -> 14.6 us  [kicks(): pl.pallas_call(kick_kernel, grid_spec=pltpu.PrefetchScalarGridSpec(num_sc...]
    pallas_call x2, Pallas kernels: 21.8 us -> 18.1 us  [amplitudes(): pl.pallas_call(amplitude_kernel, grid_spec=pltpu.PrefetchScalarGridSpec(n...]
    unnamed x20 -> x22, local copies, waits for them, and re-layouts: 4.47 us -> 4.55 us
  transfers between devices with their start and end apart: 14 -> 14, of which waited for: 1 -> 1; matrix products, arithmetic and copies ran while one was open for 0% -> 1% of each run, Pallas kernels for 57% -> 52%
where the time goes in v2:
time: 126 us; the launch traced here: 125 us
  Pallas kernels  66.7 us (53%)
  starting transfers between devices  52.1 us (41%)
  local copies, waits for them, and re-layouts  5.28 us (4%)
    all_to_all x6, starting transfers between devices, to_all(): return lax.all_to_all(value, axes, 0, 0, tiled=True)  43.9 us
    pallas_call x4, Pallas kernels, pair_step(): pl.pallas_call(functools.partial(pair_kernel, step, kicked, gathers, last...  32.4 us
    pallas_call x2, Pallas kernels, amplitudes(): pl.pallas_call(amplitude_kernel, grid_spec=pltpu.PrefetchScalarGridSpec(n...  18.1 us
    pallas_call x2, Pallas kernels, kicks(): pl.pallas_call(kick_kernel, grid_spec=pltpu.PrefetchScalarGridSpec(num_sc...  14.6 us
    ppermute x8, starting transfers between devices, exchange(): return (lax.ppermute(tail, 'sp', right), lax.ppermute(head, 'sp', left))  8.24 us
    unnamed x22, local copies, waits for them, and re-layouts  4.55 us
  transfers between devices with their start and end apart: 14, of which 1 were waited for; matrix products, arithmetic and copies ran while one was open for 1% of the time, Pallas kernels for 52%

profile of v2, /device:TPU:8, one launch (start us, length us, event | category | flops | bytes accessed | tf_op | source)
XLA Modules:
  0.0 125.1 jit_solution(18335322685008309811)
XLA Ops:
  0.6 0.0 copy-start
  0.6 0.0 copy-start.1
  0.7 0.0 copy-start.3
  0.7 1.1 copy_bitcast_fusion
  1.8 0.0 copy-start.2
  1.8 0.0 copy-done
  1.8 0.0 copy-done.1
  1.8 0.0 copy-done.3
  1.8 0.6 copy-done.2
  2.4 1.0 pack.1
  3.5 1.6 %collective-permute-start = (f32[4,4096]{1,0:T(4,128)S(1)}, f32[4,4096]{1,0:T(4,128)S(1)}, u32[]{:S(2)}, u32[]{:S(2)}) collective-permute-start(f32[4,4096]{1,0:T(4,128)S(1)} %get-tuple-element.23), channel_id=1, source_target_pairs={{0,1},{1,2},{2,3},{3,4},{4,5},{5,6},{6,7},{7,0},{8,9},{9,10},{10,1... | collective-permute-start | bytes 196616 | tf_op jit(solution)/shard_map/ppermute | solution.py:616
  5.1 0.4 collective-permute-start.1
  5.5 6.4 %all-to-all-start = ((f32[8,4,256]{2,1,0:T(4,128)}), f32[8,4,256]{2,1,0:T(4,128)S(1)}, u32[]{:S(2)}, u32[]{:S(2)}) async-start(f32[8,4,256]{2,1,0:T(4,128)} %get-tuple-element.31), calls=%async_computation | async-start | bytes 65536 | tf_op jit(solution)/shard_map/all_to_all | solution.py:620
  11.9 0.0 copy-done.5
  11.9 0.1 copy.23
  12.0 0.0 copy-start.6
  12.0 0.1 reshape.22.refs_0_
  12.2 0.5 copy-done.6
  12.7 0.1 stack.12
  12.8 0.0 copy-start.7
  12.8 0.6 copy-done.7
  13.4 0.1 stack.13
  13.6 0.1 rev.3
  13.7 0.1 copy.26
  13.8 0.1 copy.25
  13.9 0.1 reshape.24.shell_ref
  14.0 0.0 collective-permute-done.refs_3_
  14.0 0.0 collective-permute-done.1.refs_4_
  14.0 0.0 copy-start.4
  14.0 7.8 %pair_step.4 = (f32[8,8192]{1,0:T(8,128)S(1)}, f32[4,4096]{1,0:T(4,128)S(1)}, f32[4,4096]{1,0:T(4,128)S(1)}) custom-call(s32[1024]{0:T(1024)S(1)} %reshape.22.refs_0_, s32[1]{0:T(128)} %bitcast.refs_1_.position_ref, f32[8,8192]{1,0:T(8,128)S(1)} %get-tuple-element.22.refs_2_, f32[4,4096]{1,0:T(4,128)S(1)} %collective-permute-done.refs_3_, ...), custom_call_target="tpu_custom_call" | custom-call | flops 6000000000 | bytes 2000000 | tf_op jit(solution)/shard_map/pair_step/pallas_call | solution.py:329
  21.9 1.5 %collective-permute-start.2 = (f32[4,4096]{1,0:T(4,128)S(1)}, f32[4,4096]{1,0:T(4,128)S(1)}, u32[]{:S(2)}, u32[]{:S(2)}) collective-permute-start(f32[4,4096]{1,0:T(4,128)S(1)} %get-tuple-element.26), channel_id=1, source_target_pairs={{0,1},{1,2},{2,3},{3,4},{4,5},{5,6},{6,7},{7,0},{8,9},{9,10},{10,1... | collective-permute-start | bytes 196616 | tf_op jit(solution)/shard_map/ppermute | solution.py:616
  23.4 0.6 collective-permute-start.3
  23.9 0.0 all-to-all-done.point_ref
  24.0 0.0 copy-done.4
  24.0 9.1 %amplitudes.2 = (f32[13,4,8,128]{3,2,1,0:T(8,128)S(1)}, f32[128,128]{1,0:T(8,128)}) custom-call(s32[1]{0:T(128)} %bitcast.refs_1_.position_ref, f32[8,4,256]{2,1,0:T(4,128)S(1)} %all-to-all-done.point_ref, f32[8,8,128]{2,1,0:T(8,128)S(1)} %copy-done.4), custom_call_target="tpu_custom_call" | custom-call | flops 10000000000 | bytes 1000000 | tf_op jit(solution)/shard_map/amplitudes/pallas_call | solution.py:479
  33.0 9.9 %all-to-all-start.1 = ((f32[128,1,128]{2,1,0:T(1,128)}), f32[128,1,128]{2,1,0:T(1,128)S(1)}, u32[]{:S(2)}, u32[]{:S(2)}) async-start(f32[128,1,128]{2,1,0:T(1,128)} %bitcast.2), calls=%async_computation.1 | async-start | bytes 131072 | tf_op jit(solution)/shard_map/all_to_all | solution.py:620
  42.9 0.0 collective-permute-done.2.refs_3_
  42.9 0.0 collective-permute-done.3.refs_4_
  42.9 8.7 %pair_step.5 = (f32[8,8192]{1,0:T(8,128)S(1)}, f32[4,4096]{1,0:T(4,128)S(1)}, f32[4,4096]{1,0:T(4,128)S(1)}, f32[8,4,256]{2,1,0:T(4,128)}) custom-call(s32[1024]{0:T(1024)S(1)} %reshape.22.refs_0_, s32[1]{0:T(128)} %bitcast.refs_1_.position_ref, f32[8,8192]{1,0:T(8,128)S(1)} %get-tuple-element.25.refs_2_, f32[4,4096]{1,0:T(4,128)S(1)} %collective-permute-done.2.refs_3_, ...), custom_call_target="tpu_custom_call" | custom-call | flops 6000000000 | bytes 2000000 | tf_op jit(solution)/shard_map/pair_step/pallas_call | solution.py:329
  51.6 0.1 all-to-all-done.1
  51.7 5.8 %all-to-all-start.3 = ((f32[8,4,256]{2,1,0:T(4,128)}), f32[8,4,256]{2,1,0:T(4,128)S(1)}, u32[]{:S(2)}, u32[]{:S(2)}) async-start(f32[8,4,256]{2,1,0:T(4,128)} %get-tuple-element.39), calls=%async_computation.3 | async-start | bytes 65536 | tf_op jit(solution)/shard_map/all_to_all | solution.py:620
  57.6 7.3 %kicks.2 = f32[8,3,256]{2,1,0:T(4,128)} custom-call(s32[1]{0:T(128)} %bitcast.refs_1_.position_ref, f32[8,4,256]{2,1,0:T(4,128)S(1)} %all-to-all-done.point_ref, f32[8,8,128]{2,1,0:T(8,128)S(1)} %copy-done.4, f32[13,4,8,128]{3,2,1,0:T(8,128)S(1)} %get-tuple-element.32.amp_ref, f32[128,128]{1,0:T(8,128)S(1)} %bitcast.24, f32[2,128]{1,0:T(2,128)S(1)} %reshape.24.shell_ref), custom_call_target="tpu_custom_call" | custom-call | flops 10000000000 | bytes 1000000 | tf_op jit(solution)/shard_map/kicks/pallas_call | solution.py:588
  64.9 1.5 %collective-permute-start.4 = (f32[4,4096]{1,0:T(4,128)S(1)}, f32[4,4096]{1,0:T(4,128)S(1)}, u32[]{:S(2)}, u32[]{:S(2)}) collective-permute-start(f32[4,4096]{1,0:T(4,128)S(1)} %get-tuple-element.29), channel_id=1, source_target_pairs={{0,1},{1,2},{2,3},{3,4},{4,5},{5,6},{6,7},{7,0},{8,9},{9,10},{10,1... | collective-permute-start | bytes 196616 | tf_op jit(solution)/shard_map/ppermute | solution.py:616
  66.4 0.5 collective-permute-start.5
  66.9 0.0 all-to-all-done.3.point_ref
  66.9 5.7 %all-to-all-start.2 = ((f32[8,3,256]{2,1,0:T(4,128)}), f32[8,3,256]{2,1,0:T(4,128)S(1)}, u32[]{:S(2)}, u32[]{:S(2)}) async-start(f32[8,3,256]{2,1,0:T(4,128)} %kicks.2), calls=%async_computation.2 | async-start | bytes 65536 | tf_op jit(solution)/shard_map/all_to_all | solution.py:620
  72.6 9.1 %amplitudes.3 = (f32[13,4,8,128]{3,2,1,0:T(8,128)S(1)}, f32[128,128]{1,0:T(8,128)}) custom-call(s32[1]{0:T(128)} %bitcast.refs_1_.position_ref, f32[8,4,256]{2,1,0:T(4,128)S(1)} %all-to-all-done.3.point_ref, f32[8,8,128]{2,1,0:T(8,128)S(1)} %copy-done.4), custom_call_target="tpu_custom_call" | custom-call | flops 10000000000 | bytes 1000000 | tf_op jit(solution)/shard_map/amplitudes/pallas_call | solution.py:479
  81.7 0.0 all-to-all-done.2.refs_7_
  81.7 9.5 %all-to-all-start.4 = ((f32[128,1,128]{2,1,0:T(1,128)}), f32[128,1,128]{2,1,0:T(1,128)S(1)}, u32[]{:S(2)}, u32[]{:S(2)}) async-start(f32[128,1,128]{2,1,0:T(1,128)} %bitcast.9), calls=%async_computation.4 | async-start | bytes 131072 | tf_op jit(solution)/shard_map/all_to_all | solution.py:620
  91.2 0.0 collective-permute-done.4.refs_3_
  91.2 0.0 collective-permute-done.5.refs_4_
  91.2 8.2 %pair_step.6 = (f32[8,8192]{1,0:T(8,128)S(1)}, f32[4,4096]{1,0:T(4,128)S(1)}, f32[4,4096]{1,0:T(4,128)S(1)}) custom-call(s32[1024]{0:T(1024)S(1)} %reshape.22.refs_0_, s32[1]{0:T(128)} %bitcast.refs_1_.position_ref, f32[8,8192]{1,0:T(8,128)S(1)} %get-tuple-element.28.refs_2_, f32[4,4096]{1,0:T(4,128)S(1)} %collective-permute-done.4.refs_3_, ...), custom_call_target="tpu_custom_call" | custom-call | flops 6000000000 | bytes 2000000 | tf_op jit(solution)/shard_map/pair_step/pallas_call | solution.py:329
  99.4 1.5 %collective-permute-start.6 = (f32[4,4096]{1,0:T(4,128)S(1)}, f32[4,4096]{1,0:T(4,128)S(1)}, u32[]{:S(2)}, u32[]{:S(2)}) collective-permute-start(f32[4,4096]{1,0:T(4,128)S(1)} %get-tuple-element.35), channel_id=1, source_target_pairs={{0,1},{1,2},{2,3},{3,4},{4,5},{5,6},{6,7},{7,0},{8,9},{9,10},{10,1... | collective-permute-start | bytes 196616 | tf_op jit(solution)/shard_map/ppermute | solution.py:616
  100.9 0.6 collective-permute-start.7
  101.5 0.0 all-to-all-done.4
  101.5 7.3 %kicks.3 = f32[8,3,256]{2,1,0:T(4,128)} custom-call(s32[1]{0:T(128)} %bitcast.refs_1_.position_ref, f32[8,4,256]{2,1,0:T(4,128)S(1)} %all-to-all-done.3.point_ref, f32[8,8,128]{2,1,0:T(8,128)S(1)} %copy-done.4, f32[13,4,8,128]{3,2,1,0:T(8,128)S(1)} %get-tuple-element.40.amp_ref, f32[128,128]{1,0:T(8,128)S(1)} %bitcast.23, f32[2,128]{1,0:T(2,128)S(1)} %reshape.24.shell_ref), custom_call_target="tpu_custom_call" | custom-call | flops 10000000000 | bytes 1000000 | tf_op jit(solution)/shard_map/kicks/pallas_call | solution.py:588
  108.8 6.6 %all-to-all-start.5 = ((f32[8,3,256]{2,1,0:T(4,128)}), f32[8,3,256]{2,1,0:T(4,128)S(1)}, u32[]{:S(2)}, u32[]{:S(2)}) async-start(f32[8,3,256]{2,1,0:T(4,128)} %kicks.3), calls=%async_computation.5 | async-start | bytes 65536 | tf_op jit(solution)/shard_map/all_to_all | solution.py:620
  115.4 0.0 collective-permute-done.6.refs_3_
  115.4 0.0 collective-permute-done.7.refs_4_
  115.4 7.8 %pair_step.7 = (f32[3,8192]{1,0:T(4,128)S(1)}, f32[3,8192]{1,0:T(4,128)S(1)}) custom-call(s32[1024]{0:T(1024)S(1)} %reshape.22.refs_0_, s32[1]{0:T(128)} %bitcast.refs_1_.position_ref, f32[8,8192]{1,0:T(8,128)S(1)} %get-tuple-element.34.refs_2_, f32[4,4096]{1,0:T(4,128)S(1)} %collective-permute-done.6.refs_3_, f32[4,4096]{1,0:T(4,128)S(1)} %collective-permute-done.7.refs_4_), custom_call_target="tpu_custom_call" | custom-call | flops 6000000000 | bytes 2000000 | tf_op jit(solution)/shard_map/pair_step/pallas_call | solution.py:329
  123.2 0.0 all-to-all-done.5.kick_ref
  123.2 0.5 finish.1
  123.6 0.7 copy.30
  124.4 0.7 copy.29
  (7 shorter events, 0.1 us)
Async XLA Ops:
  0.6 1.1 copy-start
  0.6 1.1 copy-start.1
  0.7 1.1 copy-start.3
  1.8 0.7 copy-start.2
  3.5 10.5 %collective-permute-start = (f32[4,4096]{1,0:T(4,128)S(1)}, f32[4,4096]{1,0:T(4,128)S(1)}, u32[]{:S(2)}, u32[]{:S(2)}) collective-permute-start(f32[4,4096]{1,0:T(4,128)S(1)} %get-tuple-element.23), channel_id=1, source_target_pairs={{0,1},{1,2},{2,3},{3,4},{4,5},{5,6},{6,7},{7,0},{8,9},{9,10},{10,1... | collective-permute-start | bytes 196616 | tf_op jit(solution)/shard_map/ppermute | solution.py:616
  5.1 9.0 %collective-permute-start.1 = (f32[4,4096]{1,0:T(4,128)S(1)}, f32[4,4096]{1,0:T(4,128)S(1)}, u32[]{:S(2)}, u32[]{:S(2)}) collective-permute-start(f32[4,4096]{1,0:T(4,128)S(1)} %get-tuple-element.24), channel_id=1, source_target_pairs={{1,0},{2,1},{3,2},{4,3},{5,4},{6,5},{7,6},{0,7},{9,8},{10,9},{11,1... | collective-permute-start | bytes 196616 | tf_op jit(solution)/shard_map/ppermute | solution.py:616
  5.5 6.4 %copy-start.5 = (s32[1,4,64,4]{2,3,1,0:T(4,128)S(1)}, s32[1,4,64,4]{2,3,1,0:T(4,128)}, u32[]{:S(2)}) copy-start(s32[1,4,64,4]{2,3,1,0:T(4,128)} %param.14) | copy-start | bytes 12292
  5.5 18.4 %all-to-all-start = ((f32[8,4,256]{2,1,0:T(4,128)}), f32[8,4,256]{2,1,0:T(4,128)S(1)}, u32[]{:S(2)}, u32[]{:S(2)}) async-start(f32[8,4,256]{2,1,0:T(4,128)} %get-tuple-element.31), calls=%async_computation | async-start | bytes 65536 | tf_op jit(solution)/shard_map/all_to_all | solution.py:620
  12.0 0.7 copy-start.6
  12.8 0.7 copy-start.7
  14.0 9.9 %copy-start.4 = (f32[8,8,128]{2,1,0:T(8,128)S(1)}, f32[8,8,128]{2,1,0:T(8,128)}, u32[]{:S(2)}) copy-start(f32[8,8,128]{2,1,0:T(8,128)} %constant.9.clone.dir_ref) | copy-start | bytes 98308
  21.9 21.0 %collective-permute-start.2 = (f32[4,4096]{1,0:T(4,128)S(1)}, f32[4,4096]{1,0:T(4,128)S(1)}, u32[]{:S(2)}, u32[]{:S(2)}) collective-permute-start(f32[4,4096]{1,0:T(4,128)S(1)} %get-tuple-element.26), channel_id=1, source_target_pairs={{0,1},{1,2},{2,3},{3,4},{4,5},{5,6},{6,7},{7,0},{8,9},{9,10},{10,1... | collective-permute-start | bytes 196616 | tf_op jit(solution)/shard_map/ppermute | solution.py:616
  23.4 19.5 %collective-permute-start.3 = (f32[4,4096]{1,0:T(4,128)S(1)}, f32[4,4096]{1,0:T(4,128)S(1)}, u32[]{:S(2)}, u32[]{:S(2)}) collective-permute-start(f32[4,4096]{1,0:T(4,128)S(1)} %get-tuple-element.27), channel_id=1, source_target_pairs={{1,0},{2,1},{3,2},{4,3},{5,4},{6,5},{7,6},{0,7},{9,8},{10,9},{11,1... | collective-permute-start | bytes 196616 | tf_op jit(solution)/shard_map/ppermute | solution.py:616
  33.0 18.7 %all-to-all-start.1 = ((f32[128,1,128]{2,1,0:T(1,128)}), f32[128,1,128]{2,1,0:T(1,128)S(1)}, u32[]{:S(2)}, u32[]{:S(2)}) async-start(f32[128,1,128]{2,1,0:T(1,128)} %bitcast.2), calls=%async_computation.1 | async-start | bytes 131072 | tf_op jit(solution)/shard_map/all_to_all | solution.py:620
  51.7 15.2 %all-to-all-start.3 = ((f32[8,4,256]{2,1,0:T(4,128)}), f32[8,4,256]{2,1,0:T(4,128)S(1)}, u32[]{:S(2)}, u32[]{:S(2)}) async-start(f32[8,4,256]{2,1,0:T(4,128)} %get-tuple-element.39), calls=%async_computation.3 | async-start | bytes 65536 | tf_op jit(solution)/shard_map/all_to_all | solution.py:620
  64.9 26.3 %collective-permute-start.4 = (f32[4,4096]{1,0:T(4,128)S(1)}, f32[4,4096]{1,0:T(4,128)S(1)}, u32[]{:S(2)}, u32[]{:S(2)}) collective-permute-start(f32[4,4096]{1,0:T(4,128)S(1)} %get-tuple-element.29), channel_id=1, source_target_pairs={{0,1},{1,2},{2,3},{3,4},{4,5},{5,6},{6,7},{7,0},{8,9},{9,10},{10,1... | collective-permute-start | bytes 196616 | tf_op jit(solution)/shard_map/ppermute | solution.py:616
  66.4 24.8 %collective-permute-start.5 = (f32[4,4096]{1,0:T(4,128)S(1)}, f32[4,4096]{1,0:T(4,128)S(1)}, u32[]{:S(2)}, u32[]{:S(2)}) collective-permute-start(f32[4,4096]{1,0:T(4,128)S(1)} %get-tuple-element.30), channel_id=1, source_target_pairs={{1,0},{2,1},{3,2},{4,3},{5,4},{6,5},{7,6},{0,7},{9,8},{10,9},{11,1... | collective-permute-start | bytes 196616 | tf_op jit(solution)/shard_map/ppermute | solution.py:616
  66.9 14.8 %all-to-all-start.2 = ((f32[8,3,256]{2,1,0:T(4,128)}), f32[8,3,256]{2,1,0:T(4,128)S(1)}, u32[]{:S(2)}, u32[]{:S(2)}) async-start(f32[8,3,256]{2,1,0:T(4,128)} %kicks.2), calls=%async_computation.2 | async-start | bytes 65536 | tf_op jit(solution)/shard_map/all_to_all | solution.py:620
  81.7 19.8 %all-to-all-start.4 = ((f32[128,1,128]{2,1,0:T(1,128)}), f32[128,1,128]{2,1,0:T(1,128)S(1)}, u32[]{:S(2)}, u32[]{:S(2)}) async-start(f32[128,1,128]{2,1,0:T(1,128)} %bitcast.9), calls=%async_computation.4 | async-start | bytes 131072 | tf_op jit(solution)/shard_map/all_to_all | solution.py:620
  99.4 16.0 %collective-permute-start.6 = (f32[4,4096]{1,0:T(4,128)S(1)}, f32[4,4096]{1,0:T(4,128)S(1)}, u32[]{:S(2)}, u32[]{:S(2)}) collective-permute-start(f32[4,4096]{1,0:T(4,128)S(1)} %get-tuple-element.35), channel_id=1, source_target_pairs={{0,1},{1,2},{2,3},{3,4},{4,5},{5,6},{6,7},{7,0},{8,9},{9,10},{10,1... | collective-permute-start | bytes 196616 | tf_op jit(solution)/shard_map/ppermute | solution.py:616
  100.9 14.5 %collective-permute-start.7 = (f32[4,4096]{1,0:T(4,128)S(1)}, f32[4,4096]{1,0:T(4,128)S(1)}, u32[]{:S(2)}, u32[]{:S(2)}) collective-permute-start(f32[4,4096]{1,0:T(4,128)S(1)} %get-tuple-element.36), channel_id=1, source_target_pairs={{1,0},{2,1},{3,2},{4,3},{5,4},{6,5},{7,6},{0,7},{9,8},{10,9},{11,1... | collective-permute-start | bytes 196616 | tf_op jit(solution)/shard_map/ppermute | solution.py:616
  108.8 14.4 %all-to-all-start.5 = ((f32[8,3,256]{2,1,0:T(4,128)}), f32[8,3,256]{2,1,0:T(4,128)S(1)}, u32[]{:S(2)}, u32[]{:S(2)}) async-start(f32[8,3,256]{2,1,0:T(4,128)} %kicks.3), calls=%async_computation.5 | async-start | bytes 65536 | tf_op jit(solution)/shard_map/all_to_all | solution.py:620
